TPU v7x, 128 devices: a whole 4x4x4 slice. The times are simulated.
128 devices in a mesh: gy: 8 (over x, core), gz: 16 (over y, z).
Axes of the slice: x: 4, y: 4, z: 4, core: 2. Of those that a mesh axis runs over, the one named last changes fastest.
Arguments:
- offsets: float32 [3, 1048576], P(None, ('gy', 'gz')), may hold values from 0 to 1
- masses: float32 [1048576], P(('gy', 'gz')), may hold values from 0.25 to 4
- velocities: float32 [3, 1048576], P(None, ('gy', 'gz')), may hold values from -5 to 5
- destination: int32 [1048576, 1], P(('gy', 'gz')), may hold values from 0 to 127; in each aligned block of 8192 rows (0 to 8191, 8192 to 16383, ...) at most 128 rows name the same one
- first_weight: bfloat16 [16, 4, 3, 3, 3], replicated, may hold values from -0.625 to 0.625
- first_bias: float32 [16], replicated, may hold values from -3 to 3
- second_weight: bfloat16 [16, 16, 3, 3, 3], replicated, may hold values from -0.3125 to 0.3125
- second_bias: float32 [16], replicated, may hold values from -3 to 3
- cotangent: bfloat16 [16, 64, 128, 128], P(None, 'gy', 'gz'), may hold values from -6 to 6
Outputs:
- refined: bfloat16 [16, 64, 128, 128], P(None, 'gy', 'gz')
- grad_field: float32 [4, 64, 128, 128], P(None, 'gy', 'gz')
- grad_first_weight: float32 [16, 4, 3, 3, 3], replicated
- grad_first_bias: float32 [16], replicated
- grad_second_weight: float32 [16, 16, 3, 3, 3], replicated
- grad_second_bias: float32 [16], replicated
Inputs may be any that keep to these rules, and one draw needn't show every extreme that they name: `destination`: in the rows of one device (aligned blocks of 8192 rows) no block number is named by more than 128 rows, and some block number is named by exactly 128.
All inputs are finite; a program needn't handle non-finite values.
Results may differ from a plain program's by a relative error of at most 0.009.
Values may be sent and summed in bfloat16 or wider, within the bound.
A program may use at most 192 MiB of HBM per device.

v0:
```python
import math

import jax
import jax.numpy as jnp
from jax import lax
from jax.sharding import PartitionSpec as P


def extended_2(cells, sides, width):
    for axis, dim in sides:
        count = lax.axis_size(axis)
        ends = count - 1
        head = lax.slice_in_dim(cells, 0, width, axis=dim)
        tail = lax.slice_in_dim(cells, cells.shape[dim] - width, cells.shape[dim], axis=dim)
        cells = jnp.concatenate(
            [
                lax.ppermute(tail, axis, [(i, (i + 1) % count) for i in range(ends)]),
                cells,
                lax.ppermute(head, axis, [((i + 1) % count, i) for i in range(ends)]),
            ],
            axis=dim,
        )
    return cells


def shifted(value, axis, steps):
    count = lax.axis_size(axis)
    initial, last = (max(0, -steps), min(count, count - steps))
    return lax.ppermute(value, axis, [(source, source + steps) for source in range(initial, last)])


def cell_split(coord, span):
    position = coord * span
    cell = jnp.minimum(jnp.floor(position).astype(jnp.int32), span - 1)
    frac = position - cell.astype(position.dtype)
    return (cell, frac)


def deposit_local(arrived, span_y, span_z, span_x):
    cell_y, frac_y = cell_split(arrived[0], span_y)
    cell_z, frac_z = cell_split(arrived[1], span_z)
    cell_x, frac_x = cell_split(arrived[2], span_x)
    charges = jnp.concatenate([arrived[3:4], arrived[3:4] * arrived[4:7]], axis=0)
    grid_y, grid_z, grid_x = (span_y + 1, span_z + 1, span_x + 1)
    total = jnp.zeros((charges.shape[0], grid_y * grid_z * grid_x), jnp.float32)
    for step_y in range(2):
        weight_y = frac_y if step_y else 1.0 - frac_y
        for step_z in range(2):
            weight_z = frac_z if step_z else 1.0 - frac_z
            for step_x in range(2):
                weight_x = frac_x if step_x else 1.0 - frac_x
                index = ((cell_y + step_y) * grid_z + (cell_z + step_z)) * grid_x + cell_x + step_x
                total = total.at[:, index].add(charges * (weight_y * weight_z * weight_x)[None, :])
    return total.reshape(charges.shape[0], grid_y, grid_z, grid_x)[:, :, :, :span_x]


def conv_rims(field):
    return extended_2(field, (("gy", 1), ("gz", 2)), 1)


def pad_depth(field):
    return jnp.pad(field, ((0, 0), (0, 0), (0, 0), (1, 1)))


def conv_valid(source_ext, kernel):
    source_pad = pad_depth(source_ext)
    out_y = source_pad.shape[1] - 2
    out_z = source_pad.shape[2] - 2
    out_x = source_pad.shape[3] - 2
    result = jnp.zeros((kernel.shape[0], out_y, out_z, out_x), jnp.float32)
    for shift_y in range(3):
        for shift_z in range(3):
            for shift_x in range(3):
                window = source_pad[
                    :,
                    shift_y : shift_y + out_y,
                    shift_z : shift_z + out_z,
                    shift_x : shift_x + out_x,
                ]
                result = result + jnp.einsum(
                    "oc,cyzx->oyzx",
                    kernel[:, :, shift_y, shift_z, shift_x],
                    window,
                    preferred_element_type=jnp.float32,
                )
    return result


def flipped(kernel):
    return jnp.flip(kernel, (2, 3, 4)).transpose(1, 0, 2, 3, 4)


def dsilu(value):
    sig = jax.nn.sigmoid(value)
    return sig * (1.0 + value * (1.0 - sig))


def tap_products(delta, source_ext):
    source_pad = pad_depth(source_ext)
    span_y, span_z, span_x = (delta.shape[1], delta.shape[2], delta.shape[3])
    planes = []
    for shift_y in range(3):
        rows_out = []
        for shift_z in range(3):
            cols_out = []
            for shift_x in range(3):
                window = source_pad[
                    :,
                    shift_y : shift_y + span_y,
                    shift_z : shift_z + span_z,
                    shift_x : shift_x + span_x,
                ]
                cols_out.append(
                    jnp.einsum("oyzx,cyzx->oc", delta, window, preferred_element_type=jnp.float32)
                )
            rows_out.append(jnp.stack(cols_out, axis=-1))
        planes.append(jnp.stack(rows_out, axis=-2))
    return jnp.stack(planes, axis=-3)


def local(
    offsets,
    masses,
    velocities,
    destination,
    first_weight,
    first_bias,
    second_weight,
    second_bias,
    cotangent,
):
    count_y = lax.axis_size("gy")
    count_z = lax.axis_size("gz")
    devices = count_y * count_z
    particle_count = masses.shape[0]
    capacity = 2 * particle_count // devices
    span_y, span_z, span_x = (cotangent.shape[1], cotangent.shape[2], cotangent.shape[3])
    target = destination[:, 0]
    order = jnp.argsort(target, stable=True)
    sorted_target = target[order]
    starts = jnp.searchsorted(sorted_target, jnp.arange(devices, dtype=jnp.int32))
    ranked = jnp.arange(particle_count, dtype=jnp.int32) - starts[sorted_target]
    column = sorted_target * capacity + ranked
    filler = jnp.zeros((1, particle_count), jnp.float32)
    payload = jnp.concatenate([offsets, masses[None, :], velocities, filler], axis=0)[:, order]
    outgoing = jnp.zeros((8, devices * capacity), jnp.float32).at[:, column].set(payload)
    arrived = lax.all_to_all(
        outgoing.reshape(8, devices, capacity),
        ("gy", "gz"),
        split_axis=1,
        concat_axis=1,
        tiled=True,
    )
    arrived = arrived.reshape(8, devices * capacity)
    extended = deposit_local(arrived, span_y, span_z, span_x)
    from_below = shifted(extended[:, span_y : span_y + 1], "gy", 1)
    partial_value = jnp.concatenate([extended[:, 0:1] + from_below, extended[:, 1:span_y]], axis=1)
    from_left = shifted(partial_value[:, :, span_z : span_z + 1], "gz", 1)
    field = jnp.concatenate(
        [partial_value[:, :, 0:1] + from_left, partial_value[:, :, 1:span_z]], axis=2
    )
    density_own = field.astype(jnp.bfloat16)
    density_ext = conv_rims(density_own)
    pre_one = conv_valid(density_ext, first_weight) + first_bias[:, None, None, None]
    active = jax.nn.silu(pre_one).astype(jnp.bfloat16)
    active_ext = conv_rims(active)
    pre_two = conv_valid(active_ext, second_weight) + second_bias[:, None, None, None]
    refined = jax.nn.silu(pre_two).astype(jnp.bfloat16)
    delta_two = (cotangent.astype(jnp.float32) * dsilu(pre_two)).astype(jnp.bfloat16)
    delta_two_ext = conv_rims(delta_two)
    back_one = conv_valid(delta_two_ext, flipped(second_weight))
    delta_one = (back_one * dsilu(pre_one)).astype(jnp.bfloat16)
    delta_one_ext = conv_rims(delta_one)
    grad_field = conv_valid(delta_one_ext, flipped(first_weight))
    second_terms = tap_products(delta_two, active_ext)
    second_bias_terms = jnp.sum(delta_two, axis=(1, 2, 3), dtype=jnp.float32)
    first_terms = tap_products(delta_one, density_ext)
    first_bias_terms = jnp.sum(delta_one, axis=(1, 2, 3), dtype=jnp.float32)
    totals = lax.psum(
        (first_terms, first_bias_terms, second_terms, second_bias_terms), ("gy", "gz")
    )
    scale = 1.0 / math.sqrt(span_y * span_z * span_x * devices)
    return (
        refined,
        grad_field,
        totals[0] * scale,
        totals[1] * scale,
        totals[2] * scale,
        totals[3] * scale,
    )


def solution(mesh):
    placed = (
        P(None, ("gy", "gz")),
        P(("gy", "gz")),
        P(None, ("gy", "gz")),
        P(("gy", "gz"), None),
        P(),
        P(),
        P(),
        P(),
        P(None, "gy", "gz", None),
    )
    return jax.shard_map(
        local,
        mesh=mesh,
        in_specs=placed,
        out_specs=(P(None, "gy", "gz", None), P(None, "gy", "gz", None), P(), P(), P(), P()),
        check_vma=False,
    )
```

profile of v0, /device:TPU:1, one launch (start us, length us, event | category | flops | bytes accessed | tf_op | source)
XLA Modules:
  0.0 1301.5 jit_solution(17355583994236163222)
XLA Ops:
  0.7 7.6 sort.17
  8.2 45.5 %gather_fusion.1 = s32[8192]{0:T(1024)S(1)} fusion(s32[8192]{0:T(1024)S(1)} %bitcast.1503, s32[8192]{0:T(1024)S(1)} %fusion.281), kind=kCustom, calls=%fused_computation.1 | custom fusion | bytes 98304 | tf_op jit(solution)/shard_map/gather | solution.py:140
  53.8 17.0 %while.24 = (s32[]{:T(128)}, u32[128]{0:T(128)S(1)}, u32[128]{0:T(128)S(1)}, s32[8192]{0:T(1024)S(1)}, s32[]{:T(128)}, /*index=5*/s32[]{:T(128)}, s32[]{}) while((s32[]{:T(128)}, u32[128]{0:T(128)S(1)}, u32[128]{0:T(128)S(1)}, s32[8192]{0:T(1024)S(1)}, s32[]{:T(128)}, /*index=5*/s32[]{:T(128)}, s32[]{}) %tuple.88), condition=%wide.region_2.3_spmd.clone, body=%wide.region_1.2_spmd.clone.sunk | while | flops 2692 | bytes 10348 | solution.py:141
  53.8 1.1 gather_fusion
  55.1 1.1 gather_fusion
  56.3 1.1 gather_fusion
  57.5 1.1 gather_fusion
  70.9 48.9 %gather_fusion.2 = s32[8192]{0:T(1024)S(1)} fusion(s32[128]{0:T(128)S(1)} %convert_element_type.322, s32[8192]{0:T(1024)S(1)} %broadcast_clamp_fusion), kind=kCustom, calls=%fused_computation.2 | custom fusion | bytes 98304 | tf_op jit(solution)/shard_map/gather | solution.py:142
  120.1 2.6 copy.35
  122.7 70.2 %scatter_custom_fusion = f32[8,16384]{0,1:T(8,128)} fusion(s32[8192]{0:T(1024)S(1)} %bitcast.1529, f32[8,8192]{0,1:T(8,128)} %copy.35, s32[8192]{0:T(1024)S(1)} %fusion.281, f32[]{:T(128)} %constant.35.clone.1), kind=kCustom, calls=%fused_computation.21 | custom fusion | bytes 524800 | tf_op jit(solution)/shard_map/scatter | solution.py:146
  192.9 5.4 copy.36
  198.3 25.4 %all_to_all.5 = f32[8,128,128]{2,0,1:T(8,128)S(1)} all-to-all(f32[8,128,128]{2,0,1:T(8,128)S(1)} %copy.36), channel_id=1, replica_groups=mesh['gy'=8,'gz'=16] {'gy','gz'}, dimensions={1} | all-to-all | bytes 1048576 | tf_op jit(solution)/shard_map/all_to_all | solution.py:147
  224.4 5.0 copy.41
  229.8 5.0 copy.42
  234.8 5.0 copy.43
  239.8 5.0 copy.44
  244.8 5.0 copy.45
  249.8 5.0 copy.46
  254.8 5.0 copy.47
  259.8 5.0 copy.48
  265.5 103.8 %scatter_custom_fusion.1 = f32[4,10449]{0,1:T(8,128)} fusion(s32[16384]{0:T(1024)S(1)} %bitcast.1527, f32[16384,4]{1,0:T(8,128)} %copy.41, f32[]{:T(128)} %constant.35.clone.1), kind=kCustom, calls=%fused_computation.24 | custom fusion | flops 65536 | bytes 167696 | tf_op jit(solution)/shard_map/scatter-add | solution.py:53
  369.4 103.4 %scatter_fusion = f32[4,10449]{0,1:T(8,128)} fusion(f32[4,10449]{0,1:T(8,128)} %scatter_custom_fusion.1, s32[16384]{0:T(1024)S(1)} %bitcast.1516, f32[16384,4]{1,0:T(8,128)} %copy.42), kind=kCustom, calls=%fused_computation.6 | custom fusion | flops 65536 | bytes 851968 | tf_op jit(solution)/shard_map/scatter-add | solution.py:53
  472.9 103.1 %scatter_fusion.1 = f32[4,10449]{0,1:T(8,128)} fusion(f32[4,10449]{0,1:T(8,128)} %scatter_fusion, s32[16384]{0:T(1024)S(1)} %bitcast.1519, f32[16384,4]{1,0:T(8,128)} %copy.43), kind=kCustom, calls=%fused_computation.7 | custom fusion | flops 65536 | bytes 851968 | tf_op jit(solution)/shard_map/scatter-add | solution.py:53
  576.0 103.1 %scatter_fusion.2 = f32[4,10449]{0,1:T(8,128)} fusion(f32[4,10449]{0,1:T(8,128)} %scatter_fusion.1, s32[16384]{0:T(1024)S(1)} %bitcast.1515, f32[16384,4]{1,0:T(8,128)} %copy.44), kind=kCustom, calls=%fused_computation.8 | custom fusion | flops 65536 | bytes 851968 | tf_op jit(solution)/shard_map/scatter-add | solution.py:53
  679.0 103.1 %scatter_fusion.3 = f32[4,10449]{0,1:T(8,128)} fusion(f32[4,10449]{0,1:T(8,128)} %scatter_fusion.2, s32[16384]{0:T(1024)S(1)} %bitcast.1518, f32[16384,4]{1,0:T(8,128)} %copy.45), kind=kCustom, calls=%fused_computation.9 | custom fusion | flops 65536 | bytes 851968 | tf_op jit(solution)/shard_map/scatter-add | solution.py:53
  782.1 103.1 %scatter_fusion.4 = f32[4,10449]{0,1:T(8,128)} fusion(f32[4,10449]{0,1:T(8,128)} %scatter_fusion.3, s32[16384]{0:T(1024)S(1)} %bitcast.1514, f32[16384,4]{1,0:T(8,128)} %copy.46), kind=kCustom, calls=%fused_computation.10 | custom fusion | flops 65536 | bytes 851968 | tf_op jit(solution)/shard_map/scatter-add | solution.py:53
  885.1 103.2 %scatter_fusion.5 = f32[4,10449]{0,1:T(8,128)} fusion(f32[4,10449]{0,1:T(8,128)} %scatter_fusion.4, s32[16384]{0:T(1024)S(1)} %bitcast.1517, f32[16384,4]{1,0:T(8,128)} %copy.47), kind=kCustom, calls=%fused_computation.11 | custom fusion | flops 65536 | bytes 851968 | tf_op jit(solution)/shard_map/scatter-add | solution.py:53
  988.4 103.1 %scatter_fusion.6 = f32[4,10449]{0,1:T(8,128)} fusion(f32[4,10449]{0,1:T(8,128)} %scatter_fusion.5, s32[16384]{0:T(1024)S(1)} %bitcast.1513, f32[16384,4]{1,0:T(8,128)} %copy.48), kind=kCustom, calls=%fused_computation.12 | custom fusion | flops 65536 | bytes 851968 | tf_op jit(solution)/shard_map/scatter-add | solution.py:53
  1091.4 3.4 copy.49
  1095.2 1.9 collective-permute-start
  1098.3 9.7 collective-permute-start.1
  1108.9 2.9 collective-permute-start.3
  1111.8 3.8 collective-permute-start.2
  1116.4 1.3 collective-permute-start.5
  1117.7 5.4 collective-permute-start.4
  1132.0 1.9 collective-permute-start.7
  1133.9 5.0 collective-permute-start.6
  1140.0 1.3 collective-permute-start.9
  1141.3 14.3 %collective-permute-start.8 = (bf16[16,10,1,128]{3,0,2,1:T(8,128)(2,1)S(1)}, bf16[16,10,1,128]{3,0,2,1:T(8,128)(2,1)S(1)}, u32[]{:S(2)}, u32[]{:S(2)}) collective-permute-start(bf16[16,10,1,128]{3,0,2,1:T(8,128)(2,1)S(1)} %get-tuple-element.149), channel_id=1, source_target_pairs={{0,1},{1,2},{2,3},{3,4},{4,5},{5,6},{6,7},{7,8},{8,9},{9,10},{10,1... | collective-permute-start | bytes 122888 | tf_op jit(solution)/shard_map/ppermute | solution.py:17
  1170.2 1.9 collective-permute-start.11
  1172.1 5.1 collective-permute-start.10
  1178.2 1.3 collective-permute-start.13
  1179.5 4.8 collective-permute-start.12
  1197.8 1.9 collective-permute-start.15
  1199.7 5.1 collective-permute-start.14
  1205.6 80.8 %all-reduce.4 = (f32[16,4,3,3,3]{0,1,4,3,2:T(4,128)S(1)}, f32[16]{0:T(128)S(1)}, f32[16,16,3,3,3]{1,0,4,3,2:T(8,128)S(1)}, f32[16]{0:T(128)S(1)}) all-reduce(f32[16,4,3,3,3]{0,1,4,3,2:T(4,128)S(1)} %pad_maximum_fusion.18, f32[16]{0:T(128)S(1)} %get-tuple-element.191, ...), channel_id=1, replica_groups=mesh['gy'=8,'gz'=16] {'gy','gz'}, use_global_device_ids=true, to_apply=%region_12.13 | all-reduce | flops 8672 | bytes 69376 | tf_op jit(solution)/shard_map/psum | solution.py:179
  1288.3 1.3 collective-permute-start.17
  1289.6 4.3 collective-permute-start.16
  (330 shorter events, 65.0 us)
Async XLA Ops:
  0.6 7.6 copy-start
  70.9 49.1 %copy-start.2 = (f32[3,8192]{1,0:T(4,128)S(1)}, f32[3,8192]{1,0:T(4,128)}, u32[]{:S(2)}) copy-start(f32[3,8192]{1,0:T(4,128)} %param.13) | copy-start | bytes 294916
  70.9 49.1 %copy-start.3 = (f32[3,8192]{1,0:T(4,128)S(1)}, f32[3,8192]{1,0:T(4,128)}, u32[]{:S(2)}) copy-start(f32[3,8192]{1,0:T(4,128)} %param.11) | copy-start | bytes 294916
  70.9 49.0 %copy-start.5 = (f32[8192]{0:T(1024)S(1)}, f32[8192]{0:T(1024)}, u32[]{:S(2)}) copy-start(f32[8192]{0:T(1024)} %param.12) | copy-start | bytes 98308
  988.3 127.3 %copy-start.1 = (bf16[16,16,3,3,3]{1,0,4,3,2:T(8,128)(2,1)S(1)}, bf16[16,16,3,3,3]{1,0,4,3,2:T(8,128)(2,1)}, u32[]{:S(2)}) copy-start(bf16[16,16,3,3,3]{1,0,4,3,2:T(8,128)(2,1)} %param.17) | copy-start | bytes 41476
  1091.4 32.7 %copy-start.4 = (bf16[16,4,3,3,3]{0,1,4,3,2:T(4,128)(2,1)S(1)}, bf16[16,4,3,3,3]{0,1,4,3,2:T(4,128)(2,1)}, u32[]{:S(2)}) copy-start(bf16[16,4,3,3,3]{0,1,4,3,2:T(4,128)(2,1)} %param.15) | copy-start | bytes 10372
  1095.2 3.1 collective-permute-start
  1098.3 10.5 collective-permute-start.1
  1108.9 6.8 collective-permute-start.3
  1111.8 4.5 collective-permute-start.2
  1116.4 6.7 collective-permute-start.5
  1117.7 6.2 collective-permute-start.4
  1129.0 2.6 copy-start.6
  1132.0 7.0 collective-permute-start.7
  1133.9 6.1 collective-permute-start.6
  1140.0 15.7 %collective-permute-start.9 = (bf16[16,10,1,128]{3,0,2,1:T(8,128)(2,1)S(1)}, bf16[16,10,1,128]{3,0,2,1:T(8,128)(2,1)S(1)}, u32[]{:S(2)}, u32[]{:S(2)}) collective-permute-start(bf16[16,10,1,128]{3,0,2,1:T(8,128)(2,1)S(1)} %get-tuple-element.150), channel_id=1, source_target_pairs={{1,0},{2,1},{3,2},{4,3},{5,4},{6,5},{7,6},{8,7},{9,8},{10,9},{11,1... | collective-permute-start | bytes 122888 | tf_op jit(solution)/shard_map/ppermute | solution.py:19
  1141.3 15.2 %collective-permute-start.8 = (bf16[16,10,1,128]{3,0,2,1:T(8,128)(2,1)S(1)}, bf16[16,10,1,128]{3,0,2,1:T(8,128)(2,1)S(1)}, u32[]{:S(2)}, u32[]{:S(2)}) collective-permute-start(bf16[16,10,1,128]{3,0,2,1:T(8,128)(2,1)S(1)} %get-tuple-element.149), channel_id=1, source_target_pairs={{0,1},{1,2},{2,3},{3,4},{4,5},{5,6},{6,7},{7,8},{8,9},{9,10},{10,1... | collective-permute-start | bytes 122888 | tf_op jit(solution)/shard_map/ppermute | solution.py:17
  1161.2 1.8 copy-start.7
  1161.3 1.8 copy-start.8
  1170.2 7.6 collective-permute-start.11
  1172.1 6.1 collective-permute-start.10
  1178.2 6.9 collective-permute-start.13
  1179.5 5.7 collective-permute-start.12
  1197.8 90.4 %collective-permute-start.15 = (bf16[16,1,8,128]{3,0,2,1:T(8,128)(2,1)S(1)}, bf16[16,1,8,128]{3,0,2,1:T(8,128)(2,1)S(1)}, u32[]{:S(2)}, u32[]{:S(2)}) collective-permute-start(bf16[16,1,8,128]{3,0,2,1:T(8,128)(2,1)S(1)} %get-tuple-element.160), channel_id=1, source_target_pairs={{16,0},{32,16},{48,32},{64,48},{80,64},{96,80},{112,96},{17,1},{33... | collective-permute-start | bytes 98312 | tf_op jit(solution)/shard_map/ppermute | solution.py:19
  1199.7 88.5 %collective-permute-start.14 = (bf16[16,1,8,128]{3,0,2,1:T(8,128)(2,1)S(1)}, bf16[16,1,8,128]{3,0,2,1:T(8,128)(2,1)S(1)}, u32[]{:S(2)}, u32[]{:S(2)}) collective-permute-start(bf16[16,1,8,128]{3,0,2,1:T(8,128)(2,1)S(1)} %get-tuple-element.159), channel_id=1, source_target_pairs={{0,16},{16,32},{32,48},{48,64},{64,80},{80,96},{96,112},{1,17},{17... | collective-permute-start | bytes 98312 | tf_op jit(solution)/shard_map/ppermute | solution.py:17
  1288.3 6.1 collective-permute-start.17
  1289.6 5.1 collective-permute-start.16
where the time goes:
time: 1310 us; the launch traced here: 1300 us
  other arithmetic  840 us (64%)
  local copies, waits for them, and re-layouts  235 us (18%)
  blocking collectives  106 us (8%)
  starting transfers between devices  73.2 us (6%)
  matrix products  38.5 us (3%)
    scatter-add x8, other arithmetic, deposit_local(): total.at[:, index].add(charges * (weight_y * weight_z * weight_x)[None, :])  826 us
    psum x1, blocking collectives, local(): lax.psum((first_terms, first_bias_terms, second_terms, second_bias_terms)...  80.8 us
    scatter x1, local copies, waits for them, and re-layouts, local(): jnp.zeros((8, devices * capacity), jnp.float32).at[:, column].set(payload)  70.2 us
    gather x1, local copies, waits for them, and re-layouts, local(): ranked = jnp.arange(particle_count, dtype=jnp.int32) - starts[sorted_target]  48.9 us
    ppermute x8, starting transfers between devices, extended_2(): lax.ppermute(tail, axis, [(i, (i + 1) % count) for i in range(ends)])  47.8 us
    gather x1, local copies, waits for them, and re-layouts, local(): sorted_target = target[order]  45.5 us
    mul x8, local copies, waits for them, and re-layouts, deposit_local(): charges * (weight_y * weight_z * weight_x)[None, :]  40.1 us
  transfers between devices with their start and end apart: 18, of which 8 were waited for; matrix products, arithmetic and copies ran while one was open for 0% of the time, Pallas kernels for 0%

commit v1 on v0

v1 whole, which is shorter than its diff:
```python
import functools
import math

import jax
import jax.numpy as jnp
from jax import lax
from jax.experimental import pallas as pl
from jax.experimental.pallas import tpu as pltpu
from jax.sharding import PartitionSpec as P

F32 = jnp.float32
BF = jnp.bfloat16
MESH = pl.DeviceIdType.MESH
NT = (((1,), (1,)), ((), ()))
TN = (((0,), (0,)), ((), ()))
NN = (((1,), (0,)), ((), ()))
VMEM = pl.BlockSpec(memory_space=pltpu.VMEM)
SMEM = pl.BlockSpec(memory_space=pltpu.SMEM)
LIMIT = 62 * 1024 * 1024


def dot(a, b, dims=NN):
    return lax.dot_general(a, b, dims, preferred_element_type=F32)


def iota(shape, dim):
    return lax.broadcasted_iota(jnp.int32, shape, dim)


def halves(value):
    high = value.astype(BF)
    return high, (value - high.astype(F32)).astype(BF)


def pack_body(chunk, off, mass, vel, dest, out, acc):
    blocks, _, slots = out.shape
    count = off.shape[1]
    rows = iota((blocks, chunk), 0)
    ranks = iota((slots, chunk), 0).astype(F32)
    before = (iota((chunk, chunk), 0) < iota((chunk, chunk), 1)).astype(F32).astype(BF)
    acc[...] = jnp.zeros_like(acc)

    def step(k, base):
        here = pl.ds(pl.multiple_of(k * chunk, chunk), chunk)
        hot = (rows == dest[:, here]).astype(F32)
        hot16 = hot.astype(BF)
        earlier = dot(hot16, before) + base
        rank = jnp.sum(hot * earlier, axis=0, keepdims=True)
        place = (ranks == rank).astype(F32).astype(BF)
        spot = off[:, here]
        m = mass[:, here]
        v = vel[:, here]
        planes = (
            halves(spot[2:3] * 128.0)
            + halves(spot[0:1] * 8.0)
            + halves(spot[1:2] * 8.0)
            + (m.astype(BF), (m * v[0:1]).astype(BF), (m * v[1:2]).astype(BF), (m * v[2:3]).astype(BF))
        )
        spread = jnp.concatenate([place * plane for plane in planes], axis=0)
        acc[...] += dot(hot16, spread, NT)
        return base + jnp.sum(hot, axis=1, keepdims=True)

    lax.fori_loop(0, count // chunk, step, jnp.zeros((blocks, 1), F32))

    def plane(i):
        return acc[:, i * slots : (i + 1) * slots]

    for i in range(3):
        out[:, i, :] = plane(2 * i) + plane(2 * i + 1)
    out[:, 3, :] = jnp.zeros((blocks, slots), F32)
    for i in range(4):
        out[:, 4 + i, :] = plane(6 + i)


def pack(off, mass, vel, dest, blocks, slots):
    return pl.pallas_call(
        functools.partial(pack_body, 512),
        out_shape=jax.ShapeDtypeStruct((blocks, 8, slots), F32),
        in_specs=[VMEM] * 4,
        out_specs=VMEM,
        scratch_shapes=[pltpu.VMEM((blocks, 10 * slots), F32)],
        compiler_params=pltpu.CompilerParams(vmem_limit_bytes=LIMIT),
        name="pack",
    )(off, mass, vel, dest)


GROUP = 4


def hat(grid, at):
    return jnp.maximum(1.0 - jnp.abs(grid - at), 0.0)


def deposit_body(got, out, acc):
    sources = got.shape[0]
    xs = iota((128, 128), 0).astype(F32)
    zs = (iota((40, 128), 0) >> 2).astype(F32)
    ys = iota((16, 128), 0).astype(F32)
    upper = iota((8, 128), 0) >= 4
    acc[...] = jnp.zeros_like(acc)

    def factors(s):
        t = got[s]
        wx = hat(xs, t[0:1]).astype(BF)
        q = jnp.where(upper, t, pltpu.roll(t, 4, 0))
        wzq = hat(zs, t[2:3]) * jnp.concatenate([q] * 5, axis=0)
        wy = hat(ys, t[1:2])
        return wx, jnp.concatenate([wzq * wy[y : y + 1] for y in range(9)], axis=0).astype(BF)

    def step(k, carry):
        pairs = [factors(k * GROUP + i) for i in range(GROUP)]
        right = jnp.concatenate([p[0] for p in pairs], axis=1)
        left = jnp.concatenate([p[1] for p in pairs], axis=1)
        acc[...] += dot(left, right, NT)
        return carry

    lax.fori_loop(0, sources // GROUP, step, 0)
    for y in range(9):
        out[y] = acc[y * 40 : (y + 1) * 40]


def deposit(got):
    return pl.pallas_call(
        deposit_body,
        out_shape=jax.ShapeDtypeStruct((9, 40, 128), F32),
        in_specs=[VMEM],
        out_specs=VMEM,
        scratch_shapes=[pltpu.VMEM((360, 128), F32)],
        compiler_params=pltpu.CompilerParams(vmem_limit_bytes=LIMIT),
        name="deposit",
    )(got)


Y_PART = {1: (4, 5), 0: (0, 9), -1: (0, 4)}
Z_PART = {1: (16, 24), 0: (0, 40), -1: (0, 16)}
AROUND = [(a, b) for a in (1, 0, -1) for b in (1, 0, -1) if (a, b) != (0, 0)]
C_FROM = {1: (6, 2), 0: (0, 8), -1: (0, 2)}
C_INTO = {1: 0, 0: 2, -1: 10}


def halo_body(ny, nz, part, cot, *rest):
    got, cext = rest[:8], rest[8]
    send, receive, own = rest[9:]
    me_y, me_z = lax.axis_index("gy"), lax.axis_index("gz")
    barrier = pltpu.get_barrier_semaphore()

    def device(a, b):
        return (lax.rem(me_y + a + ny, ny), lax.rem(me_z + b + nz, nz))

    for a, b in AROUND:
        pl.semaphore_signal(barrier, inc=1, device_id=device(a, b), device_id_type=MESH)
    mine = pltpu.make_async_copy(cot, cext.at[pl.ds(2, 8), pl.ds(2, 8)], own)
    mine.start()
    pl.semaphore_wait(barrier, 8)
    copies = []
    for i, (a, b) in enumerate(AROUND):
        copies.append(
            pltpu.make_async_remote_copy(
                src_ref=part.at[pl.ds(*Y_PART[a]), pl.ds(*Z_PART[b])],
                dst_ref=got[i],
                send_sem=send.at[i],
                recv_sem=receive.at[i],
                device_id=device(a, b),
                device_id_type=MESH,
            )
        )
        copies.append(
            pltpu.make_async_remote_copy(
                src_ref=cot.at[pl.ds(*C_FROM[a]), pl.ds(*C_FROM[b])],
                dst_ref=cext.at[pl.ds(C_INTO[a], C_FROM[a][1]), pl.ds(C_INTO[b], C_FROM[b][1])],
                send_sem=send.at[8 + i],
                recv_sem=receive.at[8 + i],
                device_id=device(a, b),
                device_id_type=MESH,
            )
        )
    for c in copies:
        c.start()
    mine.wait()
    for c in copies:
        c.wait()


def halo(part, cot, ny, nz):
    return pl.pallas_call(
        functools.partial(halo_body, ny, nz),
        out_shape=[jax.ShapeDtypeStruct((Y_PART[a][1], Z_PART[b][1], 128), F32) for a, b in AROUND]
        + [jax.ShapeDtypeStruct((12, 12, 16, 128), BF)],
        in_specs=[VMEM] * 2,
        out_specs=[VMEM] * 9,
        scratch_shapes=[
            pltpu.SemaphoreType.DMA((16,)),
            pltpu.SemaphoreType.DMA((16,)),
            pltpu.SemaphoreType.DMA,
        ],
        compiler_params=pltpu.CompilerParams(collective_id=1, has_side_effects=True),
        name="halo",
    )(part, cot)


def tables_body(w1, w2, t1, t2, t2f, t1f):
    lane256, lane128 = iota((16, 256), 1), iota((16, 128), 1)
    rep16 = ((lane256 & 15) == iota((16, 256), 0)).astype(F32).astype(BF)
    rep4 = ((iota((4, 128), 1) & 3) == iota((4, 128), 0)).astype(F32).astype(BF)
    lane8 = iota((8, 256), 1)

    def tap(y, z, x):
        return (y * 3 + z) * 3 + x

    def back(y, z, x):
        return tap(2 - y, 2 - z, 2 - x)

    taps = [(y, z) for y in range(3) for z in range(3)]
    for x in range(3):
        r2 = {(y, z): dot(w2[tap(y, z, x)], rep16) for y, z in taps}
        r2f = {(y, z): dot(w2[back(y, z, x)], rep16, TN) for y, z in taps}
        r1 = {(y, z): dot(w1[tap(y, z, x)], rep4, TN) for y, z in taps}
        r1f = {
            (y, z): jnp.concatenate([dot(w1[back(y, z, x)], rep16), jnp.zeros((4, 256), F32)], axis=0)
            for y, z in taps
        }
        for oy in range(2):
            for oz in range(2):
                a = jnp.zeros((16, 256), F32)
                b = jnp.zeros((16, 256), F32)
                c = jnp.zeros((8, 256), F32)
                for y, z in taps:
                    block = (oy + y) * 4 + oz + z
                    a = jnp.where((lane256 >> 4) == block, r2[y, z], a)
                    b = jnp.where((lane256 >> 4) == block, r2f[y, z], b)
                    c = jnp.where((lane8 >> 4) == block, r1f[y, z], c)
                row = (x * 4 + oy * 2 + oz) * 16
                t2[row : row + 16] = a.astype(BF)
                t2f[row : row + 16] = b.astype(BF)
                t1f[row // 2 : row // 2 + 8] = c
            for oz in range(4):
                a = jnp.zeros((16, 128), F32)
                for y, z in taps:
                    a = jnp.where((lane128 >> 2) == (oy + y) * 8 + oz + z, r1[y, z], a)
                row = (x * 8 + oy * 4 + oz) * 16
                t1[row : row + 16] = a.astype(BF)


def tables(w1, w2):
    return pl.pallas_call(
        tables_body,
        out_shape=[
            jax.ShapeDtypeStruct((384, 128), BF),
            jax.ShapeDtypeStruct((192, 256), BF),
            jax.ShapeDtypeStruct((192, 256), BF),
            jax.ShapeDtypeStruct((96, 256), F32),
        ],
        in_specs=[VMEM] * 2,
        out_specs=[VMEM] * 4,
        compiler_params=pltpu.CompilerParams(vmem_limit_bytes=LIMIT),
        name="tables",
    )(w1, w2)


def unet_body(
    ny,
    nz,
    pos,
    part,
    bl,
    bo,
    br,
    sl,
    sr,
    al,
    ao,
    ar,
    cext,
    t1,
    t2,
    t2f,
    t1f,
    b1,
    b2,
    refined,
    field,
    sums,
    dens,
    act,
    ds1,
    d2,
    d1,
    g2,
    g1,
    s2,
    s1,
):
    gy, gz = pos[0], pos[1]
    lane = iota((128, 128), 1)
    not_first, not_last = lane > 0, lane < 127

    def from_left(v):
        return jnp.where(not_first[: v.shape[0]], pltpu.roll(v, 1, 1), 0.0)

    def from_right(v):
        return jnp.where(not_last[: v.shape[0]], pltpu.roll(v, 127, 1), 0.0)

    def along_x(v, rows, j):
        cols = slice(j * 128, (j + 1) * 128)
        return from_left(v[:rows, cols]) + v[rows : 2 * rows, cols] + from_right(v[2 * rows :, cols])

    zrow = (iota((80, 128), 0) >> 2) - 5 + gz * 8
    z_inside = (zrow >= 0) & (zrow < nz * 8)

    from_side = (gz > 0).astype(F32)
    from_below = (gy > 0).astype(F32)

    def across(left, own, right):
        return jnp.concatenate(
            [
                left[0:16],
                own[0:8] + left[16:24] * from_side,
                own[8:32],
                right[0:8] + own[32:40],
                right[8:16],
            ],
            axis=0,
        )

    for y in range(16):
        if y < 4:
            slab = across(bl[y], bo[y], br[y])
        elif y < 12:
            slab = across(sl[y - 4], part[y - 4], sr[y - 4])
            if y == 4:
                slab = slab + across(bl[4], bo[4], br[4]) * from_below
        else:
            slab = across(al[y - 12], ao[y - 12], ar[y - 12])
            if y == 12:
                slab = slab + across(sl[8], part[8], sr[8])
        slab = jnp.concatenate([slab, jnp.zeros((16, 128), F32)], axis=0)
        slab = pltpu.roll(slab, 4, 0)
        at = gy * 8 + (y - 4)
        inside = z_inside & ((at >= 0) & (at < ny * 8))
        dens[y] = jnp.where(inside, slab, 0.0).astype(BF)

    def spread_bias(ref, times):
        return jnp.concatenate([jnp.broadcast_to(ref[...], (16, 128))] * times, axis=0)

    bias1, bias2 = spread_bias(b1, 8), spread_bias(b2, 4)

    row1 = iota((128, 128), 0)

    def conv1(by, carry):
        right = jnp.concatenate(
            [
                jnp.concatenate([dens[2 * by + y, 16 * j : 16 * j + 32, :] for y in range(4)], axis=0)
                for j in range(4)
            ],
            axis=1,
        )
        out = dot(t1[...], right)
        yy = gy * 8 + 2 * by - 3 + (row1 >> 6)
        y_in = (yy >= 0) & (yy < ny * 8)
        for j in range(4):
            pre = along_x(out, 128, j) + bias1
            sig = jax.nn.sigmoid(pre)
            zz = gz * 8 + 4 * j - 4 + ((row1 >> 4) & 3)
            inside = y_in & (zz >= 0) & (zz < nz * 8)
            value = jnp.where(inside, pre * sig, 0.0).astype(BF)
            act[pl.ds(2 * by, 2), 4 * j : 4 * j + 4] = value.reshape(2, 4, 16, 128)
            slope = jnp.where(inside, sig * (1.0 + pre * (1.0 - sig)), 0.0)
            ds1[pl.ds(2 * by, 2), 4 * j : 4 * j + 4] = slope.reshape(2, 4, 16, 128)
        return carry

    lax.fori_loop(0, 7, conv1, 0)

    def block(ref, y0, z0):
        return jnp.concatenate([ref[y0 + y, z0 : z0 + 4].reshape(64, 128) for y in range(4)], axis=0)

    row2 = iota((64, 128), 0)

    def conv2(by, carry):
        right = jnp.concatenate([block(act, 2 * by, 2 * bz + 1) for bz in range(6)], axis=1)
        out = dot(t2[...], right)
        yy = gy * 8 + 2 * by - 2 + (row2 >> 5)
        y_in = (yy >= 0) & (yy < ny * 8)
        for bz in range(6):
            pre = along_x(out, 64, bz) + bias2
            sig = jax.nn.sigmoid(pre)
            zz = gz * 8 + 2 * bz - 2 + ((row2 >> 4) & 1)
            inside = y_in & (zz >= 0) & (zz < nz * 8)
            if 1 <= bz <= 4:

                @pl.when((by >= 1) & (by <= 4))
                def _():
                    refined[pl.ds(2 * by - 2, 2), 2 * bz - 2 : 2 * bz] = (
                        (pre * sig).astype(BF).reshape(2, 2, 16, 128)
                    )

            cot = cext[pl.ds(2 * by, 2), 2 * bz : 2 * bz + 2].reshape(64, 128).astype(F32)
            delta = jnp.where(inside, cot * (sig * (1.0 + pre * (1.0 - sig))), 0.0)
            d2[pl.ds(2 * by, 2), 2 * bz : 2 * bz + 2] = delta.astype(BF).reshape(2, 2, 16, 128)
        return carry

    lax.fori_loop(0, 6, conv2, 0)

    def conv3(by, carry):
        right = jnp.concatenate([block(d2, 2 * by, 2 * bz) for bz in range(5)], axis=1)
        out = dot(t2f[...], right)
        for bz in range(5):
            slope = ds1[pl.ds(2 * by + 2, 2), 2 * bz + 3 : 2 * bz + 5].reshape(64, 128)
            delta = along_x(out, 64, bz) * slope
            d1[pl.ds(2 * by, 2), 2 * bz : 2 * bz + 2] = delta.astype(BF).reshape(2, 2, 16, 128)
        return carry

    lax.fori_loop(0, 5, conv3, 0)

    g2[...] = jnp.zeros_like(g2)
    g1[...] = jnp.zeros_like(g1)
    s2[...] = jnp.zeros_like(s2)
    s1[...] = jnp.zeros_like(s1)
    table4 = t1f[...].astype(BF)

    def last(by, carry):
        right = jnp.concatenate([block(d1, 2 * by, 2 * bz) for bz in range(4)], axis=1)
        out = dot(table4, right)
        for bz in range(4):
            field[pl.ds(2 * by, 2), 2 * bz : 2 * bz + 2] = along_x(out, 32, bz).reshape(2, 2, 8, 128)

        lefts, rights = [], []
        for bz in range(4):
            delta = d2[pl.ds(2 * by + 2, 2), 2 * bz + 2 : 2 * bz + 4].reshape(64, 128).astype(F32)
            s2[...] += delta[0:16] + delta[16:32] + delta[32:48] + delta[48:64]
            lefts.append(
                jnp.concatenate([from_right(delta), delta, from_left(delta)], axis=0).astype(BF)
            )
            rights.append(block(act, 2 * by + 2, 2 * bz + 3))
        g2[...] += dot(jnp.concatenate(lefts, axis=1), jnp.concatenate(rights, axis=1), NT)

        lefts, rights = [], []
        for j in range(2):
            delta = d1[pl.ds(2 * by + 1, 2), 4 * j + 1 : 4 * j + 5].reshape(128, 128).astype(F32)
            total = delta[0:16]
            for i in range(1, 8):
                total = total + delta[16 * i : 16 * i + 16]
            s1[...] += total
            lefts.append(
                jnp.concatenate([from_right(delta), delta, from_left(delta)], axis=0).astype(BF)
            )
            rights.append(
                jnp.concatenate(
                    [dens[2 * by + 3 + y, 16 * j + 16 : 16 * j + 48, :] for y in range(4)], axis=0
                )
            )
        g1[...] += dot(jnp.concatenate(lefts, axis=1), jnp.concatenate(rights, axis=1), NT)
        return carry

    lax.fori_loop(0, 4, last, 0)

    lane16 = iota((16, 128), 1)
    for x in range(3):
        total = g2[x * 64 : x * 64 + 16]
        for i in range(1, 4):
            shift = ((i >> 1) * 4 + (i & 1)) * 16
            total = total + pltpu.roll(g2[x * 64 + 16 * i : x * 64 + 16 * i + 16], 256 - shift, 1)
        sums[16 * x : 16 * x + 16, 0:256] = total
        total = g1[x * 128 : x * 128 + 16]
        for i in range(1, 8):
            shift = (i >> 2) * 32 + (i & 3) * 4
            total = total + pltpu.roll(g1[x * 128 + 16 * i : x * 128 + 16 * i + 16], 128 - shift, 1)
        if x == 0:
            total = jnp.where(lane16 == 96, jnp.sum(s1[...], axis=1, keepdims=True), total)
            total = jnp.where(lane16 == 97, jnp.sum(s2[...], axis=1, keepdims=True), total)
        sums[16 * x : 16 * x + 16, 256:384] = total


def unet(ny, nz, *args):
    return pl.pallas_call(
        functools.partial(unet_body, ny, nz),
        out_shape=[
            jax.ShapeDtypeStruct((8, 8, 16, 128), BF),
            jax.ShapeDtypeStruct((8, 8, 8, 128), F32),
            jax.ShapeDtypeStruct((48, 384), F32),
        ],
        in_specs=[SMEM] + [VMEM] * 16,
        out_specs=[VMEM] * 3,
        scratch_shapes=[
            pltpu.VMEM((16, 80, 128), BF),
            pltpu.VMEM((14, 16, 16, 128), BF),
            pltpu.VMEM((14, 16, 16, 128), F32),
            pltpu.VMEM((12, 12, 16, 128), BF),
            pltpu.VMEM((10, 10, 16, 128), BF),
            pltpu.VMEM((192, 256), F32),
            pltpu.VMEM((384, 128), F32),
            pltpu.VMEM((16, 128), F32),
            pltpu.VMEM((16, 128), F32),
        ],
        compiler_params=pltpu.CompilerParams(vmem_limit_bytes=LIMIT),
        name="unet",
    )(*args)


def local(off, mass, vel, dest, w1, b1, w2, b2, cot):
    ny, nz = lax.axis_size("gy"), lax.axis_size("gz")
    devices = ny * nz
    count = mass.shape[0]
    slots = 2 * count // devices
    t1, t2, t2f, t1f = tables(
        w1.transpose(2, 3, 4, 1, 0).reshape(27, 4, 16), w2.transpose(2, 3, 4, 0, 1).reshape(27, 16, 16)
    )
    sent = pack(off, mass.reshape(1, count), vel, dest.reshape(1, count), devices, slots)
    got = lax.all_to_all(sent, ("gy", "gz"), split_axis=0, concat_axis=0, tiled=True)
    part = deposit(got)
    *pieces, cext = halo(part, cot.transpose(1, 2, 0, 3), ny, nz)
    pos = jnp.stack([lax.axis_index("gy"), lax.axis_index("gz")]).astype(jnp.int32)
    refined, field, sums = unet(
        ny, nz, pos, part, *pieces, cext, t1, t2, t2f, t1f, b1.reshape(16, 1), b2.reshape(16, 1)
    )
    scale = 1.0 / math.sqrt(8 * 8 * 128 * devices)
    total = lax.psum(sums, ("gy", "gz")) * scale
    second = total[:, :256].reshape(3, 16, 4, 4, 16)[:, :, :3, :3]
    first = total[:, 256:].reshape(3, 16, 4, 8, 4)[:, :, :3, :3]
    return (
        refined.transpose(2, 0, 1, 3),
        field[:, :, :4].transpose(2, 0, 1, 3),
        first.transpose(1, 4, 2, 3, 0),
        total[:16, 256 + 96],
        second.transpose(1, 4, 2, 3, 0),
        total[:16, 256 + 97],
    )


def solution(mesh):
    placed = (
        P(None, ("gy", "gz")),
        P(("gy", "gz")),
        P(None, ("gy", "gz")),
        P(("gy", "gz"), None),
        P(),
        P(),
        P(),
        P(),
        P(None, "gy", "gz", None),
    )
    return jax.shard_map(
        local,
        mesh=mesh,
        in_specs=placed,
        out_specs=(P(None, "gy", "gz", None), P(None, "gy", "gz", None), P(), P(), P(), P()),
        check_vma=False,
    )
```

time: 1310 us -> 235 us (0.18)
  other arithmetic: 840 us -> 1.54 us
  local copies, waits for them, and re-layouts: 235 us -> 9.57 us
  waiting for transfers between devices: 5.64 us -> 143 us
  blocking collectives: 106 us -> 0 us
  starting transfers between devices: 73.2 us -> 11.5 us
  Pallas kernels: 0 us -> 54.9 us
  matrix products: 38.5 us -> 0 us
    scatter-add x8 -> x0, other arithmetic: 826 us -> none  [deposit_local(): total.at[:, index].add(charges * (weight_y * weight_z * weight_x)[None, :])]
    psum x0 -> x1, waiting for transfers between devices: none -> 135 us  [local(): total = lax.psum(sums, ('gy', 'gz')) * scale]
    gather x16 -> x0, local copies, waits for them, and re-layouts: 110 us -> none  [the longest x1 48.9 us: local(): ranked = jnp.arange(particle_count, dtype=jnp.int32) - starts[sorted_target]]
    psum x1 -> x0, blocking collectives: 80.8 us -> none  [local(): lax.psum((first_terms, first_bias_terms, second_terms, second_bias_terms)...]
    ppermute x18 -> x0, starting transfers between devices: 73.2 us -> none  [the longest x8 47.8 us: extended_2(): lax.ppermute(tail, axis, [(i, (i + 1) % count) for i in range(ends)])]
    scatter x1 -> x0, local copies, waits for them, and re-layouts: 70.2 us -> none  [local(): jnp.zeros((8, devices * capacity), jnp.float32).at[:, column].set(payload)]
    pallas_call x0 -> x5, Pallas kernels: none -> 54.9 us  [the longest x1 15.2 us: pack(): pl.pallas_call(functools.partial(pack_body, 512), out_shape=jax.ShapeDtyp...]
    mul x8 -> x0, local copies, waits for them, and re-layouts: 40.1 us -> none  [deposit_local(): charges * (weight_y * weight_z * weight_x)[None, :]]
  transfers between devices with their start and end apart: 18 -> 2, of which waited for: 8 -> 2; matrix products, arithmetic and copies ran while one was open for 0% -> 2% of each run, Pallas kernels for 0% -> 1%
where the time goes in v1:
time: 235 us; the launch traced here: 234 us
  waiting for transfers between devices  143 us (61%)
  Pallas kernels  54.9 us (23%)
  between operations  14.1 us (6%)
  starting transfers between devices  11.5 us (5%)
  local copies, waits for them, and re-layouts  9.57 us (4%)
    psum x1, waiting for transfers between devices, local(): total = lax.psum(sums, ('gy', 'gz')) * scale  135 us
    pallas_call x1, Pallas kernels, pack(): pl.pallas_call(functools.partial(pack_body, 512), out_shape=jax.ShapeDtyp...  15.2 us
    pallas_call x1, Pallas kernels, halo(): pl.pallas_call(functools.partial(halo_body, ny, nz), out_shape=[jax.Shape...  14 us
    pallas_call x1, Pallas kernels, unet(): pl.pallas_call(functools.partial(unet_body, ny, nz), out_shape=[jax.Shape...  12.5 us
    all_to_all x1, starting transfers between devices, local(): lax.all_to_all(sent, ('gy', 'gz'), split_axis=0, concat_axis=0, tiled=True)  11.5 us
    pallas_call x1, Pallas kernels, deposit(): pl.pallas_call(deposit_body, out_shape=jax.ShapeDtypeStruct((9, 40, 128),...  11 us
    all_to_all x1, waiting for transfers between devices, local(): lax.all_to_all(sent, ('gy', 'gz'), split_axis=0, concat_axis=0, tiled=True)  7.44 us
    unnamed x17, local copies, waits for them, and re-layouts  5.77 us
  transfers between devices with their start and end apart: 2, of which 2 were waited for; matrix products, arithmetic and copies ran while one was open for 2% of the time, Pallas kernels for 1%

profile of v1, /device:TPU:1, one launch (start us, length us, event | category | flops | bytes accessed | tf_op | source)
XLA Modules:
  0.0 234.1 jit_solution(13333526306173561748)
XLA Ops:
  7.2 15.2 %pack.1 = f32[128,8,128]{2,1,0:T(8,128)} custom-call(f32[3,8192]{1,0:T(4,128)} %off.1, f32[1,8192]{1,0:T(1,128)} %bitcast.29, f32[3,8192]{1,0:T(4,128)} %vel.1, s32[1,8192]{1,0:T(1,128)} %bitcast.30), custom_call_target="tpu_custom_call" | custom-call | tf_op jit(solution)/shard_map/pack/pallas_call | solution.py:76
  22.4 0.0 copy-start.2
  22.4 11.5 %all-to-all-start = ((f32[128,8,128]{2,1,0:T(8,128)}), f32[128,8,128]{2,1,0:T(8,128)S(1)}, u32[]{:S(2)}, u32[]{:S(2)}) async-start(f32[128,8,128]{2,1,0:T(8,128)} %pack.1), calls=%async_computation | async-start | bytes 1048576 | tf_op jit(solution)/shard_map/all_to_all | solution.py:508
  33.9 0.0 all-reduce.2.cloned.1.call-start
  33.9 0.0 copy-start.4
  33.9 0.6 copy-done.4
  34.6 0.7 copy.23.b1
  35.3 0.0 copy-start.5
  35.3 0.7 copy-done.5
  35.9 0.7 copy.24.b2
  36.6 0.0 copy-done.2
  36.6 0.9 copy.33
  37.5 2.2 tables.1
  39.6 0.6 pad_add_fusion.pos
  40.3 7.4 %all-to-all-done.got = f32[128,8,128]{2,1,0:T(8,128)S(1)} async-done(((f32[128,8,128]{2,1,0:T(8,128)}), f32[128,8,128]{2,1,0:T(8,128)S(1)}, u32[]{:S(2)}, u32[]{:S(2)}) %all-to-all-start) | async-done | bytes 524320 | tf_op jit(solution)/shard_map/all_to_all | solution.py:508
  47.7 0.0 copy-start
  47.7 0.8 copy-done
  48.5 11.0 %deposit.1.part = f32[9,40,128]{2,1,0:T(8,128)} custom-call(f32[128,8,128]{2,1,0:T(8,128)} %copy-done), custom_call_target="tpu_custom_call" | custom-call | tf_op jit(solution)/shard_map/deposit/pallas_call | solution.py:123
  59.6 14.0 %halo.1 = (f32[5,24,128]{2,1,0:T(8,128)}, f32[5,40,128]{2,1,0:T(8,128)}, f32[5,16,128]{2,1,0:T(8,128)}, f32[9,24,128]{2,1,0:T(8,128)}, f32[9,16,128]{2,1,0:T(8,1...) custom-call(f32[9,40,128]{2,1,0:T(8,128)} %deposit.1.part, ...), custom_call_target="tpu_custom_call" | custom-call | tf_op jit(solution)/shard_map/halo/pallas_call | solution.py:185
  73.5 12.5 %unet.1 = (bf16[8,8,16,128]{3,2,1,0:T(8,128)(2,1)}, f32[8,8,8,128]{3,2,1,0:T(8,128)}, f32[48,384]{1,0:T(8,128)}) custom-call(s32[2]{0:T(128)} %pad_add_fusion.pos, f32[9,40,128]{2,1,0:T(8,128)} %deposit.1.part, f32[5,24,128]{2,1,0:T(8,128)} %get-tuple-element.22.bl, f32[5,40,128]{2,1,0:T(8,128)} %get-tuple-element.23.bo, ...), custom_call_target="tpu_custom_call" | custom-call | tf_op jit(solution)/shard_map/unet/pallas_call | solution.py:474
  86.0 0.0 copy-start.3
  86.0 0.0 all-reduce.2.cloned.1.call-update
  86.1 1.0 slice_bitcast_fusion
  87.1 0.0 copy-done.3
  87.1 0.8 copy.27
  87.9 0.7 copy.28
  88.5 135.0 %all-reduce.2.cloned.1.call-done = f32[48,384]{1,0:T(8,128)} async-done(((f32[48,384]{1,0:T(8,128)}), f32[48,384]{1,0:T(8,128)}) %all-reduce.2.cloned.1.call-update) | async-done | bytes 73744 | tf_op jit(solution)/shard_map/psum | solution.py:516
  223.6 0.9 broadcast_multiply_fusion
  224.5 0.0 copy-start.1
  224.5 0.7 slice_reduce_fusion
  225.2 0.0 copy-done.1
  225.2 0.1 copy.25
  225.3 0.2 reshape.42
  225.4 0.0 slice-start
  225.5 0.6 copy.29
  226.1 0.2 slice-done
  226.2 0.3 reshape.43
  226.6 0.7 copy.34
  (3 shorter events, 0.0 us)
Async XLA Ops:
  22.4 14.2 %copy-start.2 = (bf16[16,8,8,128]{3,2,1,0:T(8,128)(2,1)S(1)}, bf16[16,8,8,128]{3,2,1,0:T(8,128)(2,1)}, u32[]{:S(2)}) copy-start(bf16[16,8,8,128]{3,2,1,0:T(8,128)(2,1)} %param.17) | copy-start | bytes 786436
  22.4 25.3 %all-to-all-start = ((f32[128,8,128]{2,1,0:T(8,128)}), f32[128,8,128]{2,1,0:T(8,128)S(1)}, u32[]{:S(2)}, u32[]{:S(2)}) async-start(f32[128,8,128]{2,1,0:T(8,128)} %pack.1), calls=%async_computation | async-start | bytes 1048576 | tf_op jit(solution)/shard_map/all_to_all | solution.py:508
  33.9 189.7 %all-reduce.2.cloned.1.call-start = ((), (), s32[]{:S(2)}) async-start(), calls=%async_computation.1 | async-start | bytes 147456 | tf_op jit(solution)/shard_map/psum | solution.py:516
  33.9 0.7 copy-start.4
  35.3 0.7 copy-start.5
  47.7 0.8 copy-start
  86.0 1.0 copy-start.3
  224.5 0.7 copy-start.1
  225.4 0.8 slice-start
Sparse Core Ops, SparseCore 0:
  86.2 137.3 all-reduce.1

commit v2 on v1

--- a/solution.py
+++ b/solution.py
@@ -455,19 +455,26 @@
 
     lane16 = iota((16, 128), 1)
     for x in range(3):
-        total = g2[x * 64 : x * 64 + 16]
+        wide = g2[x * 64 : x * 64 + 16]
         for i in range(1, 4):
             shift = ((i >> 1) * 4 + (i & 1)) * 16
-            total = total + pltpu.roll(g2[x * 64 + 16 * i : x * 64 + 16 * i + 16], 256 - shift, 1)
-        sums[16 * x : 16 * x + 16, 0:256] = total
-        total = g1[x * 128 : x * 128 + 16]
+            wide = wide + pltpu.roll(g2[x * 64 + 16 * i : x * 64 + 16 * i + 16], 256 - shift, 1)
+        slim = g1[x * 128 : x * 128 + 16]
         for i in range(1, 8):
             shift = (i >> 2) * 32 + (i & 3) * 4
-            total = total + pltpu.roll(g1[x * 128 + 16 * i : x * 128 + 16 * i + 16], 128 - shift, 1)
+            slim = slim + pltpu.roll(g1[x * 128 + 16 * i : x * 128 + 16 * i + 16], 128 - shift, 1)
+        low, high = wide[:, :128], wide[:, 128:]
+        free = (lane16 & 63) >= 48
+        low = jnp.where(free, jnp.where(lane16 < 64, pltpu.roll(slim, 48, 1), pltpu.roll(slim, 80, 1)), low)
+        high = jnp.where(free, pltpu.roll(slim, 112, 1), high)
         if x == 0:
-            total = jnp.where(lane16 == 96, jnp.sum(s1[...], axis=1, keepdims=True), total)
-            total = jnp.where(lane16 == 97, jnp.sum(s2[...], axis=1, keepdims=True), total)
-        sums[16 * x : 16 * x + 16, 256:384] = total
+            low = jnp.where(lane16 == 60, jnp.sum(s1[...], axis=1, keepdims=True), low)
+            low = jnp.where(lane16 == 61, jnp.sum(s2[...], axis=1, keepdims=True), low)
+        for half in range(2):
+            sums[2 * x + half] = low[8 * half : 8 * half + 8]
+            sums[6 + 2 * x + half] = high[8 * half : 8 * half + 8]
+    for i in range(12, 16):
+        sums[i] = jnp.zeros((8, 128), F32)
 
 
 def unet(ny, nz, *args):
@@ -476,7 +483,7 @@
         out_shape=[
             jax.ShapeDtypeStruct((8, 8, 16, 128), BF),
             jax.ShapeDtypeStruct((8, 8, 8, 128), F32),
-            jax.ShapeDtypeStruct((48, 384), F32),
+            jax.ShapeDtypeStruct((16, 8, 128), F32),
         ],
         in_specs=[SMEM] + [VMEM] * 16,
         out_specs=[VMEM] * 3,
@@ -496,6 +503,111 @@
     )(*args)
 
 
+def reduce_body(ny, nz, pay, out, from_z, from_y, send, receive):
+    me_y, me_z = lax.axis_index("gy"), lax.axis_index("gz")
+    barrier = pltpu.get_barrier_semaphore()
+
+    def along_z(k):
+        return (me_y, lax.rem(me_z + k, nz))
+
+    def along_y(k):
+        return (lax.rem(me_y + k, ny), me_z)
+
+    for k in range(1, nz):
+        pl.semaphore_signal(barrier, inc=1, device_id=along_z(k), device_id_type=MESH)
+    for k in range(1, ny):
+        pl.semaphore_signal(barrier, inc=1, device_id=along_y(k), device_id_type=MESH)
+    pl.semaphore_wait(barrier, nz + ny - 2)
+
+    def copy(src, dst, sem, to):
+        return pltpu.make_async_remote_copy(
+            src_ref=src,
+            dst_ref=dst,
+            send_sem=send.at[sem],
+            recv_sem=receive.at[sem],
+            device_id=to,
+            device_id_type=MESH,
+        )
+
+    first = [
+        copy(pay.at[lax.rem(me_z + k, nz)], from_z.at[k], k, along_z(k)) for k in range(1, nz)
+    ]
+    for c in first:
+        c.start()
+    for c in first:
+        c.wait()
+    total = pay[me_z]
+    for k in range(1, nz):
+        total = total + from_z[k]
+    from_y[me_y] = total
+    second = [copy(from_y.at[me_y], from_y.at[me_y], nz + k, along_y(k)) for k in range(1, ny)]
+    for c in second:
+        c.start()
+    for c in second:
+        c.wait()
+    total = from_y[0]
+    for k in range(1, ny):
+        total = total + from_y[k]
+    out[me_z] = total
+    third = [copy(out.at[me_z], out.at[me_z], nz + ny + k, along_z(k)) for k in range(1, nz)]
+    for c in third:
+        c.start()
+    for c in third:
+        c.wait()
+
+
+def reduce(pay, ny, nz):
+    return pl.pallas_call(
+        functools.partial(reduce_body, ny, nz),
+        out_shape=jax.ShapeDtypeStruct((nz, 8, 128), F32),
+        in_specs=[VMEM],
+        out_specs=VMEM,
+        scratch_shapes=[
+            pltpu.VMEM((nz, 8, 128), F32),
+            pltpu.VMEM((ny, 8, 128), F32),
+            pltpu.SemaphoreType.DMA((2 * nz + ny,)),
+            pltpu.SemaphoreType.DMA((2 * nz + ny,)),
+        ],
+        compiler_params=pltpu.CompilerParams(collective_id=2, has_side_effects=True),
+        name="reduce",
+    )(pay)
+
+
+def finish_body(scale, sums, first, bias1, second, bias2):
+    kinds = [jnp.concatenate([sums[2 * i], sums[2 * i + 1]], axis=0) * scale for i in range(6)]
+    turned = jnp.concatenate(kinds + [jnp.zeros((32, 128), F32)], axis=0).T
+    for x in range(3):
+        for y in range(3):
+            kind = x if y < 2 else 3 + x
+            base = 64 * (y & 1)
+            for z in range(3):
+                t = (y * 3 + z) * 3 + x
+                at = base + 16 * z
+                wide = pltpu.roll(kinds[kind], 128 - at, 1) if at else kinds[kind]
+                second[t] = wide[:, :16]
+                rows = turned[base + 48 + 4 * z : base + 52 + 4 * z]
+                rows = jnp.concatenate([rows, rows], axis=0)
+                slim = pltpu.roll(rows, 128 - 16 * kind, 1) if kind else rows
+                first[t] = slim[:4, :16]
+    bias1[...] = turned[60:61, :16]
+    bias2[...] = turned[61:62, :16]
+
+
+def finish(sums, scale):
+    return pl.pallas_call(
+        functools.partial(finish_body, scale),
+        out_shape=[
+            jax.ShapeDtypeStruct((27, 4, 16), F32),
+            jax.ShapeDtypeStruct((1, 16), F32),
+            jax.ShapeDtypeStruct((27, 16, 16), F32),
+            jax.ShapeDtypeStruct((1, 16), F32),
+        ],
+        in_specs=[VMEM],
+        out_specs=[VMEM] * 4,
+        name="finish",
+    )(sums)
+
+
 def local(off, mass, vel, dest, w1, b1, w2, b2, cot):
     ny, nz = lax.axis_size("gy"), lax.axis_size("gz")
     devices = ny * nz
@@ -513,16 +625,14 @@
         ny, nz, pos, part, *pieces, cext, t1, t2, t2f, t1f, b1.reshape(16, 1), b2.reshape(16, 1)
     )
     scale = 1.0 / math.sqrt(8 * 8 * 128 * devices)
-    total = lax.psum(sums, ("gy", "gz")) * scale
-    second = total[:, :256].reshape(3, 16, 4, 4, 16)[:, :, :3, :3]
-    first = total[:, 256:].reshape(3, 16, 4, 8, 4)[:, :, :3, :3]
+    first, bias1, second, bias2 = finish(reduce(sums, ny, nz), scale)
     return (
         refined.transpose(2, 0, 1, 3),
         field[:, :, :4].transpose(2, 0, 1, 3),
-        first.transpose(1, 4, 2, 3, 0),
-        total[:16, 256 + 96],
-        second.transpose(1, 4, 2, 3, 0),
-        total[:16, 256 + 97],
+        first.reshape(3, 3, 3, 4, 16).transpose(4, 3, 0, 1, 2),
+        bias1.reshape(16),
+        second.reshape(3, 3, 3, 16, 16).transpose(3, 4, 0, 1, 2),
+        bias2.reshape(16),
     )
 
 

time: 235 us -> 103 us (0.44)
  waiting for transfers between devices: 143 us -> 7.48 us
  Pallas kernels: 54.9 us -> 75.1 us
  between operations: 14.1 us -> 0.7 us
  local copies, waits for them, and re-layouts: 9.57 us -> 6.79 us
    psum x1 -> x0, waiting for transfers between devices: 135 us -> none  [local(): total = lax.psum(sums, ('gy', 'gz')) * scale]
    pallas_call x0 -> x2, Pallas kernels: none -> 20.2 us  [the longest x1 18.5 us: reduce(): pl.pallas_call(functools.partial(reduce_body, ny, nz), out_shape=jax.Shap...]
    unnamed x17 -> x13, local copies, waits for them, and re-layouts: 5.77 us -> 5.41 us
  transfers between devices with their start and end apart: 2 -> 1, of which waited for: 2 -> 1; matrix products, arithmetic and copies ran while one was open for 2% -> 3% of each run, Pallas kernels for 1% -> 2%
where the time goes in v2:
time: 103 us; the launch traced here: 102 us
  Pallas kernels  75.1 us (73%)
  starting transfers between devices  11.5 us (11%)
  waiting for transfers between devices  7.48 us (7%)
  local copies, waits for them, and re-layouts  6.79 us (7%)
    pallas_call x1, Pallas kernels, reduce(): pl.pallas_call(functools.partial(reduce_body, ny, nz), out_shape=jax.Shap...  18.5 us
    pallas_call x1, Pallas kernels, pack(): pl.pallas_call(functools.partial(pack_body, 512), out_shape=jax.ShapeDtyp...  15.2 us
    pallas_call x1, Pallas kernels, halo(): pl.pallas_call(functools.partial(halo_body, ny, nz), out_shape=[jax.Shape...  13.9 us
    pallas_call x1, Pallas kernels, unet(): pl.pallas_call(functools.partial(unet_body, ny, nz), out_shape=[jax.Shape...  12.6 us
    all_to_all x1, starting transfers between devices, local(): lax.all_to_all(sent, ('gy', 'gz'), split_axis=0, concat_axis=0, tiled=True)  11.5 us
    pallas_call x1, Pallas kernels, deposit(): pl.pallas_call(deposit_body, out_shape=jax.ShapeDtypeStruct((9, 40, 128),...  11 us
    all_to_all x1, waiting for transfers between devices, local(): lax.all_to_all(sent, ('gy', 'gz'), split_axis=0, concat_axis=0, tiled=True)  7.48 us
    unnamed x13, local copies, waits for them, and re-layouts  5.41 us
  transfers between devices with their start and end apart: 1, of which 1 were waited for; matrix products, arithmetic and copies ran while one was open for 3% of the time, Pallas kernels for 2%

profile of v2, /device:TPU:1, one launch (start us, length us, event | category | flops | bytes accessed | tf_op | source)
XLA Modules:
  0.0 102.2 jit_solution(17397828691105273261)
XLA Ops:
  0.6 15.2 %pack.1 = f32[128,8,128]{2,1,0:T(8,128)} custom-call(f32[3,8192]{1,0:T(4,128)} %off.1, f32[1,8192]{1,0:T(1,128)} %bitcast.29, f32[3,8192]{1,0:T(4,128)} %vel.1, s32[1,8192]{1,0:T(1,128)} %bitcast.30), custom_call_target="tpu_custom_call" | custom-call | tf_op jit(solution)/shard_map/pack/pallas_call | solution.py:76
  15.8 0.0 copy-start.1
  15.8 11.5 %all-to-all-start = ((f32[128,8,128]{2,1,0:T(8,128)}), f32[128,8,128]{2,1,0:T(8,128)S(1)}, u32[]{:S(2)}, u32[]{:S(2)}) async-start(f32[128,8,128]{2,1,0:T(8,128)} %pack.1), calls=%async_computation | async-start | bytes 1048576 | tf_op jit(solution)/shard_map/all_to_all | solution.py:620
  27.3 0.0 copy-start.3
  27.3 0.6 copy-done.3
  28.0 0.7 copy.16.b1
  28.7 0.0 copy-start.4
  28.7 0.7 copy-done.4
  29.3 0.7 copy.17.b2
  30.0 0.0 copy-done.1
  30.0 0.9 copy.21
  30.9 2.2 %tables.1 = (bf16[384,128]{1,0:T(8,128)(2,1)}, bf16[192,256]{1,0:T(8,128)(2,1)}, bf16[192,256]{1,0:T(8,128)(2,1)}, f32[96,256]{1,0:T(8,128)}) custom-call(bf16[27,4,16]{2,1,0:T(4,128)(2,1)} %bitcast.31, bf16[27,16,16]{2,1,0:T(8,128)(2,1)} %bitcast.28), custom_call_target="tpu_custom_call" | custom-call | tf_op jit(solution)/shard_map/tables/pallas_call | solution.py:245
  33.1 0.6 pad_add_fusion.pos
  33.7 7.5 %all-to-all-done.got = f32[128,8,128]{2,1,0:T(8,128)S(1)} async-done(((f32[128,8,128]{2,1,0:T(8,128)}), f32[128,8,128]{2,1,0:T(8,128)S(1)}, u32[]{:S(2)}, u32[]{:S(2)}) %all-to-all-start) | async-done | bytes 524320 | tf_op jit(solution)/shard_map/all_to_all | solution.py:620
  41.2 0.0 copy-start
  41.2 0.8 copy-done
  42.0 11.0 %deposit.1.part = f32[9,40,128]{2,1,0:T(8,128)} custom-call(f32[128,8,128]{2,1,0:T(8,128)} %copy-done), custom_call_target="tpu_custom_call" | custom-call | tf_op jit(solution)/shard_map/deposit/pallas_call | solution.py:123
  53.0 13.9 %halo.1 = (f32[5,24,128]{2,1,0:T(8,128)}, f32[5,40,128]{2,1,0:T(8,128)}, f32[5,16,128]{2,1,0:T(8,128)}, f32[9,24,128]{2,1,0:T(8,128)}, f32[9,16,128]{2,1,0:T(8,1...) custom-call(f32[9,40,128]{2,1,0:T(8,128)} %deposit.1.part, ...), custom_call_target="tpu_custom_call" | custom-call | tf_op jit(solution)/shard_map/halo/pallas_call | solution.py:185
  66.9 12.6 %unet.1 = (bf16[8,8,16,128]{3,2,1,0:T(8,128)(2,1)}, f32[8,8,8,128]{3,2,1,0:T(8,128)}, f32[16,8,128]{2,1,0:T(8,128)}) custom-call(s32[2]{0:T(128)} %pad_add_fusion.pos, f32[9,40,128]{2,1,0:T(8,128)} %deposit.1.part, f32[5,24,128]{2,1,0:T(8,128)} %get-tuple-element.26.bl, f32[5,40,128]{2,1,0:T(8,128)} %get-tuple-element.27.bo, ...), custom_call_target="tpu_custom_call" | custom-call | tf_op jit(solution)/shard_map/unet/pallas_call | solution.py:481
  79.5 0.0 copy-start.2
  79.5 1.8 %copy.18 = bf16[16,8,8,128]{3,2,1,0:T(8,128)(2,1)} copy(bf16[16,8,8,128]{3,0,2,1:T(8,128)(2,1)} %bitcast.27) | data formatting | bytes 524288
  81.3 18.5 %reduce.1.sums = f32[16,8,128]{2,1,0:T(8,128)} custom-call(f32[16,8,128]{2,1,0:T(8,128)} %get-tuple-element.41.pay), custom_call_target="tpu_custom_call" | custom-call | tf_op jit(solution)/shard_map/reduce/pallas_call | solution.py:560
  99.8 0.0 copy-done.2
  99.8 0.7 copy.19
  100.5 1.7 %finish.1 = (f32[27,4,16]{2,1,0:T(4,128)}, f32[1,16]{1,0:T(1,128)}, f32[27,16,16]{2,1,0:T(8,128)}, f32[1,16]{1,0:T(1,128)}) custom-call(f32[16,8,128]{2,1,0:T(8,128)} %reduce.1.sums), custom_call_target="tpu_custom_call" | custom-call | tf_op jit(solution)/shard_map/finish/pallas_call | solution.py:597
  (1 shorter events, 0.0 us)
Async XLA Ops:
  15.8 14.2 %copy-start.1 = (bf16[16,8,8,128]{3,2,1,0:T(8,128)(2,1)S(1)}, bf16[16,8,8,128]{3,2,1,0:T(8,128)(2,1)}, u32[]{:S(2)}) copy-start(bf16[16,8,8,128]{3,2,1,0:T(8,128)(2,1)} %param.17) | copy-start | bytes 786436
  15.8 25.3 %all-to-all-start = ((f32[128,8,128]{2,1,0:T(8,128)}), f32[128,8,128]{2,1,0:T(8,128)S(1)}, u32[]{:S(2)}, u32[]{:S(2)}) async-start(f32[128,8,128]{2,1,0:T(8,128)} %pack.1), calls=%async_computation | async-start | bytes 1048576 | tf_op jit(solution)/shard_map/all_to_all | solution.py:620
  27.3 0.7 copy-start.3
  28.7 0.7 copy-start.4
  41.2 0.8 copy-start
  79.5 20.2 %copy-start.2 = (f32[8,8,8,128]{3,2,1,0:T(8,128)S(1)}, f32[8,8,8,128]{3,2,1,0:T(8,128)}, u32[]{:S(2)}) copy-start(f32[8,8,8,128]{3,2,1,0:T(8,128)} %get-tuple-element.40) | copy-start | bytes 786436

commit v3 on v2

--- a/solution.py
+++ b/solution.py
@@ -72,18 +72,6 @@
         out[:, 4 + i, :] = plane(6 + i)
 
 
-def pack(off, mass, vel, dest, blocks, slots):
-    return pl.pallas_call(
-        functools.partial(pack_body, 512),
-        out_shape=jax.ShapeDtypeStruct((blocks, 8, slots), F32),
-        in_specs=[VMEM] * 4,
-        out_specs=VMEM,
-        scratch_shapes=[pltpu.VMEM((blocks, 10 * slots), F32)],
-        compiler_params=pltpu.CompilerParams(vmem_limit_bytes=LIMIT),
-        name="pack",
-    )(off, mass, vel, dest)
-
-
 GROUP = 4
 
 
@@ -91,8 +79,8 @@
     return jnp.maximum(1.0 - jnp.abs(grid - at), 0.0)
 
 
-def deposit_body(got, out, acc):
-    sources = got.shape[0]
+def deposit_body(got, acc, first_ready, ready, groups):
+    size = got.shape[0] // groups
     xs = iota((128, 128), 0).astype(F32)
     zs = (iota((40, 128), 0) >> 2).astype(F32)
     ys = iota((16, 128), 0).astype(F32)
@@ -107,28 +95,21 @@
         wy = hat(ys, t[1:2])
         return wx, jnp.concatenate([wzq * wy[y : y + 1] for y in range(9)], axis=0).astype(BF)
 
-    def step(k, carry):
-        pairs = [factors(k * GROUP + i) for i in range(GROUP)]
-        right = jnp.concatenate([p[0] for p in pairs], axis=1)
-        left = jnp.concatenate([p[1] for p in pairs], axis=1)
-        acc[...] += dot(left, right, NT)
+    def add(g):
+        for k in range(size // GROUP):
+            pairs = [factors(g * size + k * GROUP + i) for i in range(GROUP)]
+            right = jnp.concatenate([p[0] for p in pairs], axis=1)
+            left = jnp.concatenate([p[1] for p in pairs], axis=1)
+            acc[...] += dot(left, right, NT)
+
+    def step(g, carry):
+        ready(g)
+        add(g)
         return carry
 
-    lax.fori_loop(0, sources // GROUP, step, 0)
-    for y in range(9):
-        out[y] = acc[y * 40 : (y + 1) * 40]
-
-
-def deposit(got):
-    return pl.pallas_call(
-        deposit_body,
-        out_shape=jax.ShapeDtypeStruct((9, 40, 128), F32),
-        in_specs=[VMEM],
-        out_specs=VMEM,
-        scratch_shapes=[pltpu.VMEM((360, 128), F32)],
-        compiler_params=pltpu.CompilerParams(vmem_limit_bytes=LIMIT),
-        name="deposit",
-    )(got)
+    first_ready()
+    add(0)
+    lax.fori_loop(1, groups, step, 0)
 
 
 Y_PART = {1: (4, 5), 0: (0, 9), -1: (0, 4)}
@@ -136,66 +117,6 @@
 AROUND = [(a, b) for a in (1, 0, -1) for b in (1, 0, -1) if (a, b) != (0, 0)]
 C_FROM = {1: (6, 2), 0: (0, 8), -1: (0, 2)}
 C_INTO = {1: 0, 0: 2, -1: 10}
-
-
-def halo_body(ny, nz, part, cot, *rest):
-    got, cext = rest[:8], rest[8]
-    send, receive, own = rest[9:]
-    me_y, me_z = lax.axis_index("gy"), lax.axis_index("gz")
-    barrier = pltpu.get_barrier_semaphore()
-
-    def device(a, b):
-        return (lax.rem(me_y + a + ny, ny), lax.rem(me_z + b + nz, nz))
-
-    for a, b in AROUND:
-        pl.semaphore_signal(barrier, inc=1, device_id=device(a, b), device_id_type=MESH)
-    mine = pltpu.make_async_copy(cot, cext.at[pl.ds(2, 8), pl.ds(2, 8)], own)
-    mine.start()
-    pl.semaphore_wait(barrier, 8)
-    copies = []
-    for i, (a, b) in enumerate(AROUND):
-        copies.append(
-            pltpu.make_async_remote_copy(
-                src_ref=part.at[pl.ds(*Y_PART[a]), pl.ds(*Z_PART[b])],
-                dst_ref=got[i],
-                send_sem=send.at[i],
-                recv_sem=receive.at[i],
-                device_id=device(a, b),
-                device_id_type=MESH,
-            )
-        )
-        copies.append(
-            pltpu.make_async_remote_copy(
-                src_ref=cot.at[pl.ds(*C_FROM[a]), pl.ds(*C_FROM[b])],
-                dst_ref=cext.at[pl.ds(C_INTO[a], C_FROM[a][1]), pl.ds(C_INTO[b], C_FROM[b][1])],
-                send_sem=send.at[8 + i],
-                recv_sem=receive.at[8 + i],
-                device_id=device(a, b),
-                device_id_type=MESH,
-            )
-        )
-    for c in copies:
-        c.start()
-    mine.wait()
-    for c in copies:
-        c.wait()
-
-
-def halo(part, cot, ny, nz):
-    return pl.pallas_call(
-        functools.partial(halo_body, ny, nz),
-        out_shape=[jax.ShapeDtypeStruct((Y_PART[a][1], Z_PART[b][1], 128), F32) for a, b in AROUND]
-        + [jax.ShapeDtypeStruct((12, 12, 16, 128), BF)],
-        in_specs=[VMEM] * 2,
-        out_specs=[VMEM] * 9,
-        scratch_shapes=[
-            pltpu.SemaphoreType.DMA((16,)),
-            pltpu.SemaphoreType.DMA((16,)),
-            pltpu.SemaphoreType.DMA,
-        ],
-        compiler_params=pltpu.CompilerParams(collective_id=1, has_side_effects=True),
-        name="halo",
-    )(part, cot)
 
 
 def tables_body(w1, w2, t1, t2, t2f, t1f):
@@ -241,26 +162,11 @@
                 t1[row : row + 16] = a.astype(BF)
 
 
-def tables(w1, w2):
-    return pl.pallas_call(
-        tables_body,
-        out_shape=[
-            jax.ShapeDtypeStruct((384, 128), BF),
-            jax.ShapeDtypeStruct((192, 256), BF),
-            jax.ShapeDtypeStruct((192, 256), BF),
-            jax.ShapeDtypeStruct((96, 256), F32),
-        ],
-        in_specs=[VMEM] * 2,
-        out_specs=[VMEM] * 4,
-        compiler_params=pltpu.CompilerParams(vmem_limit_bytes=LIMIT),
-        name="tables",
-    )(w1, w2)
-
-
 def unet_body(
     ny,
     nz,
-    pos,
+    gy,
+    gz,
     part,
     bl,
     bo,
@@ -290,7 +196,6 @@
     s2,
     s1,
 ):
-    gy, gz = pos[0], pos[1]
     lane = iota((128, 128), 1)
     not_first, not_last = lane > 0, lane < 127
 
@@ -311,6 +216,7 @@
     from_below = (gy > 0).astype(F32)
 
     def across(left, own, right):
+        left, own, right = left.astype(F32), own.astype(F32), right.astype(F32)
         return jnp.concatenate(
             [
                 left[0:16],
@@ -326,13 +232,13 @@
         if y < 4:
             slab = across(bl[y], bo[y], br[y])
         elif y < 12:
-            slab = across(sl[y - 4], part[y - 4], sr[y - 4])
+            slab = across(sl[y - 4], part[(y - 4) * 40 : (y - 3) * 40], sr[y - 4])
             if y == 4:
                 slab = slab + across(bl[4], bo[4], br[4]) * from_below
         else:
             slab = across(al[y - 12], ao[y - 12], ar[y - 12])
             if y == 12:
-                slab = slab + across(sl[8], part[8], sr[8])
+                slab = slab + across(sl[8], part[320:360], sr[8])
         slab = jnp.concatenate([slab, jnp.zeros((16, 128), F32)], axis=0)
         slab = pltpu.roll(slab, 4, 0)
         at = gy * 8 + (y - 4)
@@ -477,47 +383,12 @@
         sums[i] = jnp.zeros((8, 128), F32)
 
 
-def unet(ny, nz, *args):
-    return pl.pallas_call(
-        functools.partial(unet_body, ny, nz),
-        out_shape=[
-            jax.ShapeDtypeStruct((8, 8, 16, 128), BF),
-            jax.ShapeDtypeStruct((8, 8, 8, 128), F32),
-            jax.ShapeDtypeStruct((16, 8, 128), F32),
-        ],
-        in_specs=[SMEM] + [VMEM] * 16,
-        out_specs=[VMEM] * 3,
-        scratch_shapes=[
-            pltpu.VMEM((16, 80, 128), BF),
-            pltpu.VMEM((14, 16, 16, 128), BF),
-            pltpu.VMEM((14, 16, 16, 128), F32),
-            pltpu.VMEM((12, 12, 16, 128), BF),
-            pltpu.VMEM((10, 10, 16, 128), BF),
-            pltpu.VMEM((192, 256), F32),
-            pltpu.VMEM((384, 128), F32),
-            pltpu.VMEM((16, 128), F32),
-            pltpu.VMEM((16, 128), F32),
-        ],
-        compiler_params=pltpu.CompilerParams(vmem_limit_bytes=LIMIT),
-        name="unet",
-    )(*args)
-
-
-def reduce_body(ny, nz, pay, out, from_z, from_y, send, receive):
-    me_y, me_z = lax.axis_index("gy"), lax.axis_index("gz")
-    barrier = pltpu.get_barrier_semaphore()
-
+def reduce_body(ny, nz, me_y, me_z, pay, out, from_z, from_y, send, receive):
     def along_z(k):
         return (me_y, lax.rem(me_z + k, nz))
 
     def along_y(k):
         return (lax.rem(me_y + k, ny), me_z)
-
-    for k in range(1, nz):
-        pl.semaphore_signal(barrier, inc=1, device_id=along_z(k), device_id_type=MESH)
-    for k in range(1, ny):
-        pl.semaphore_signal(barrier, inc=1, device_id=along_y(k), device_id_type=MESH)
-    pl.semaphore_wait(barrier, nz + ny - 2)
 
     def copy(src, dst, sem, to):
         return pltpu.make_async_remote_copy(
@@ -556,23 +427,6 @@
         c.wait()
 
 
-def reduce(pay, ny, nz):
-    return pl.pallas_call(
-        functools.partial(reduce_body, ny, nz),
-        out_shape=jax.ShapeDtypeStruct((nz, 8, 128), F32),
-        in_specs=[VMEM],
-        out_specs=VMEM,
-        scratch_shapes=[
-            pltpu.VMEM((nz, 8, 128), F32),
-            pltpu.VMEM((ny, 8, 128), F32),
-            pltpu.SemaphoreType.DMA((2 * nz + ny,)),
-            pltpu.SemaphoreType.DMA((2 * nz + ny,)),
-        ],
-        compiler_params=pltpu.CompilerParams(collective_id=2, has_side_effects=True),
-        name="reduce",
-    )(pay)
-
-
 def finish_body(scale, sums, first, bias1, second, bias2):
     kinds = [jnp.concatenate([sums[2 * i], sums[2 * i + 1]], axis=0) * scale for i in range(6)]
     turned = jnp.concatenate(kinds + [jnp.zeros((32, 128), F32)], axis=0).T
@@ -608,24 +462,176 @@
     )(sums)
 
 
+GROUPS = 16
+
+
+def step_body(ny, nz, off, mass, vel, dest, cot, w1, w2, b1, b2, refined, field, sums, *rest):
+    (sent, pile, got, part, part16, cext, t1, t2, t2f, t1f, dens, act, ds1, d2, d1, g2, g1, s2, s1) = rest[:19]
+    pieces, (pay, from_z, from_y) = rest[19:27], rest[27:30]
+    out_all, in_group, out_halo, in_halo, out_sum, in_sum = rest[30:]
+    me_y, me_z = lax.axis_index("gy"), lax.axis_index("gz")
+    devices = ny * nz
+    size = devices // GROUPS
+    barrier = pltpu.get_barrier_semaphore()
+
+    def partner(j):
+        k = lax.rem(j * 37, devices)
+        return (lax.rem(me_y + k // nz, ny), lax.rem(me_z + lax.rem(k, nz), nz))
+
+    def device(a, b):
+        return (lax.rem(me_y + a + ny, ny), lax.rem(me_z + b + nz, nz))
+
+    def greet(j, carry):
+        pl.semaphore_signal(barrier, inc=1, device_id=partner(j), device_id_type=MESH)
+        return carry
+
+    lax.fori_loop(1, devices, greet, 0)
+
+    cext[2:10, 2:10] = cot[...]
+    tables_body(w1, w2, t1, t2, t2f, t1f)
+    pack_body(512, off, mass, vel, dest, sent, pile)
+
+    pl.semaphore_wait(barrier, devices - 1)
+
+    def send(j, carry):
+        y, z = partner(j)
+        pltpu.make_async_remote_copy(
+            src_ref=sent.at[y * nz + z],
+            dst_ref=got.at[j],
+            send_sem=out_all,
+            recv_sem=in_group.at[j // size],
+            device_id=(y, z),
+            device_id_type=MESH,
+        ).start()
+        return carry
+
+    lax.fori_loop(1, devices, send, 0)
+    got[0] = sent[me_y * nz + me_z]
+
+    def halo(i, src, dst):
+        copy = pltpu.make_async_remote_copy(
+            src_ref=src,
+            dst_ref=dst,
+            send_sem=out_halo.at[i],
+            recv_sem=in_halo.at[i],
+            device_id=device(*AROUND[i % 8]),
+            device_id_type=MESH,
+        )
+        copy.start()
+        return copy
+
+    copies = [
+        halo(
+            8 + i,
+            cot.at[pl.ds(*C_FROM[a]), pl.ds(*C_FROM[b])],
+            cext.at[pl.ds(C_INTO[a], C_FROM[a][1]), pl.ds(C_INTO[b], C_FROM[b][1])],
+        )
+        for i, (a, b) in enumerate(AROUND)
+    ]
+
+    def landed(first, count, g):
+        pltpu.make_async_remote_copy(
+            src_ref=sent.at[pl.ds(0, count)],
+            dst_ref=got.at[pl.ds(first, count)],
+            send_sem=out_all,
+            recv_sem=in_group.at[g],
+            device_id=device(0, 1),
+            device_id_type=MESH,
+        ).wait_recv()
+
+    deposit_body(got, part, lambda: landed(1, size - 1, 0), lambda g: landed(g * size, size, g), GROUPS)
+    for y in range(9):
+        part16[y] = part[y * 40 : (y + 1) * 40].astype(BF)
+    copies += [
+        halo(i, part16.at[pl.ds(*Y_PART[a]), pl.ds(*Z_PART[b])], pieces[i]) for i, (a, b) in enumerate(AROUND)
+    ]
+    pltpu.make_async_remote_copy(
+        src_ref=sent.at[pl.ds(1, devices - 1)],
+        dst_ref=got.at[pl.ds(1, devices - 1)],
+        send_sem=out_all,
+        recv_sem=in_group.at[0],
+        device_id=device(0, 1),
+        device_id_type=MESH,
+    ).wait_send()
+    for c in copies:
+        c.wait()
+
+    unet_body(
+        ny, nz, me_y, me_z, part, *pieces, cext, t1, t2, t2f, t1f, b1, b2,
+        refined, field, pay, dens, act, ds1, d2, d1, g2, g1, s2, s1,
+    )
+    reduce_body(ny, nz, me_y, me_z, pay, sums, from_z, from_y, out_sum, in_sum)
+
+
+def whole_step(ny, nz, slots, *args):
+    devices = ny * nz
+    return pl.pallas_call(
+        functools.partial(step_body, ny, nz),
+        out_shape=[
+            jax.ShapeDtypeStruct((8, 8, 16, 128), BF),
+            jax.ShapeDtypeStruct((8, 8, 8, 128), F32),
+            jax.ShapeDtypeStruct((nz, 8, 128), F32),
+        ],
+        in_specs=[VMEM] * 9,
+        out_specs=[VMEM] * 3,
+        scratch_shapes=[
+            pltpu.VMEM((devices, 8, slots), F32),
+            pltpu.VMEM((devices, 10 * slots), F32),
+            pltpu.VMEM((devices, 8, slots), F32),
+            pltpu.VMEM((360, 128), F32),
+            pltpu.VMEM((9, 40, 128), BF),
+            pltpu.VMEM((12, 12, 16, 128), BF),
+            pltpu.VMEM((384, 128), BF),
+            pltpu.VMEM((192, 256), BF),
+            pltpu.VMEM((192, 256), BF),
+            pltpu.VMEM((96, 256), F32),
+            pltpu.VMEM((16, 80, 128), BF),
+            pltpu.VMEM((14, 16, 16, 128), BF),
+            pltpu.VMEM((14, 16, 16, 128), F32),
+            pltpu.VMEM((12, 12, 16, 128), BF),
+            pltpu.VMEM((10, 10, 16, 128), BF),
+            pltpu.VMEM((192, 256), F32),
+            pltpu.VMEM((384, 128), F32),
+            pltpu.VMEM((16, 128), F32),
+            pltpu.VMEM((16, 128), F32),
+        ]
+        + [pltpu.VMEM((Y_PART[a][1], Z_PART[b][1], 128), BF) for a, b in AROUND]
+        + [
+            pltpu.VMEM((nz, 8, 128), F32),
+            pltpu.VMEM((nz, 8, 128), F32),
+            pltpu.VMEM((ny, 8, 128), F32),
+            pltpu.SemaphoreType.DMA,
+            pltpu.SemaphoreType.DMA((GROUPS,)),
+            pltpu.SemaphoreType.DMA((16,)),
+            pltpu.SemaphoreType.DMA((16,)),
+            pltpu.SemaphoreType.DMA((2 * nz + ny,)),
+            pltpu.SemaphoreType.DMA((2 * nz + ny,)),
+        ],
+        compiler_params=pltpu.CompilerParams(collective_id=1, has_side_effects=True, vmem_limit_bytes=LIMIT),
+        name="step",
+    )(*args)
+
+
 def local(off, mass, vel, dest, w1, b1, w2, b2, cot):
     ny, nz = lax.axis_size("gy"), lax.axis_size("gz")
     devices = ny * nz
     count = mass.shape[0]
-    slots = 2 * count // devices
-    t1, t2, t2f, t1f = tables(
-        w1.transpose(2, 3, 4, 1, 0).reshape(27, 4, 16), w2.transpose(2, 3, 4, 0, 1).reshape(27, 16, 16)
+    scale = 1.0 / math.sqrt(8 * 8 * 128 * devices)
+    refined, field, sums = whole_step(
+        ny,
+        nz,
+        2 * count // devices,
+        off,
+        mass.reshape(1, count),
+        vel,
+        dest.reshape(1, count),
+        cot.transpose(1, 2, 0, 3),
+        w1.transpose(2, 3, 4, 1, 0).reshape(27, 4, 16),
+        w2.transpose(2, 3, 4, 0, 1).reshape(27, 16, 16),
+        b1.reshape(16, 1),
+        b2.reshape(16, 1),
     )
-    sent = pack(off, mass.reshape(1, count), vel, dest.reshape(1, count), devices, slots)
-    got = lax.all_to_all(sent, ("gy", "gz"), split_axis=0, concat_axis=0, tiled=True)
-    part = deposit(got)
-    *pieces, cext = halo(part, cot.transpose(1, 2, 0, 3), ny, nz)
-    pos = jnp.stack([lax.axis_index("gy"), lax.axis_index("gz")]).astype(jnp.int32)
-    refined, field, sums = unet(
-        ny, nz, pos, part, *pieces, cext, t1, t2, t2f, t1f, b1.reshape(16, 1), b2.reshape(16, 1)
-    )
-    scale = 1.0 / math.sqrt(8 * 8 * 128 * devices)
-    first, bias1, second, bias2 = finish(reduce(sums, ny, nz), scale)
+    first, bias1, second, bias2 = finish(sums, scale)
     return (
         refined.transpose(2, 0, 1, 3),
         field[:, :, :4].transpose(2, 0, 1, 3),

time: 103 us -> 74 us (0.72)
  starting transfers between devices: 11.5 us -> 0 us
  Pallas kernels: 75.1 us -> 66.8 us
  waiting for transfers between devices: 7.48 us -> 0 us
    all_to_all x1 -> x0, starting transfers between devices: 11.5 us -> none  [local(): lax.all_to_all(sent, ('gy', 'gz'), split_axis=0, concat_axis=0, tiled=True)]
    pallas_call x6 -> x1, Pallas kernels: 73.4 us -> 65.1 us  [whole_step(): pl.pallas_call(functools.partial(step_body, ny, nz), out_shape=[jax.Shape...]
    all_to_all x1 -> x0, waiting for transfers between devices: 7.48 us -> none  [local(): lax.all_to_all(sent, ('gy', 'gz'), split_axis=0, concat_axis=0, tiled=True)]
    unnamed x13 -> x9, local copies, waits for them, and re-layouts: 5.41 us -> 4.91 us
  transfers between devices with their start and end apart: 1 -> 0, of which waited for: 1 -> 0; matrix products, arithmetic and copies ran while one was open for 3% -> 0% of each run, Pallas kernels for 2% -> 0%
where the time goes in v3:
time: 74 us; the launch traced here: 73.7 us
  Pallas kernels  66.8 us (90%)
  local copies, waits for them, and re-layouts  6.29 us (8%)
    pallas_call x1, Pallas kernels, whole_step(): pl.pallas_call(functools.partial(step_body, ny, nz), out_shape=[jax.Shape...  65.1 us
    unnamed x9, local copies, waits for them, and re-layouts  4.91 us
    pallas_call x1, Pallas kernels, finish(): pl.pallas_call(functools.partial(finish_body, scale), out_shape=[jax.Shap...  1.72 us

profile of v3, /device:TPU:1, one launch (start us, length us, event | category | flops | bytes accessed | tf_op | source)
XLA Modules:
  0.0 73.7 jit_solution(2112469270325923028)
XLA Ops:
  0.6 0.0 copy-start.1
  0.6 0.6 copy-done.1
  1.3 0.0 copy-start.2
  1.3 0.7 copy.16.b1
  2.0 0.0 copy-done.2
  2.0 0.7 copy.17.b2
  2.7 1.8 %copy.21 = bf16[16,8,8,128]{3,0,2,1:T(8,128)(2,1)} copy(bf16[16,8,8,128]{3,2,1,0:T(8,128)(2,1)} %param.17) | data formatting | bytes 524288 | tf_op args[8]
  4.5 65.1 %step.1 = (bf16[8,8,16,128]{3,2,1,0:T(8,128)(2,1)}, f32[8,8,8,128]{3,2,1,0:T(8,128)}, f32[16,8,128]{2,1,0:T(8,128)}) custom-call(f32[3,8192]{1,0:T(4,128)} %off.1, f32[1,8192]{1,0:T(1,128)} %bitcast.27, f32[3,8192]{1,0:T(4,128)} %vel.1, s32[1,8192]{1,0:T(1,128)} %bitcast.28, bf16[8,8,16,128]{3,2,1,0:T(8,128)(2,1)} %bitcast.24, bf16[27,4,16]{2,1,0:T(4,128)(2,1)} %bitcast.29, ...), custom_call_target="tpu_custom_call" | custom-call | tf_op jit(solution)/shard_map/step/pallas_call | solution.py:568
  69.5 0.0 copy-start
  69.6 1.8 %copy.18 = bf16[16,8,8,128]{3,2,1,0:T(8,128)(2,1)} copy(bf16[16,8,8,128]{3,0,2,1:T(8,128)(2,1)} %bitcast.25) | data formatting | bytes 524288
  71.3 0.0 copy-done
  71.3 0.7 copy.19
  72.0 1.7 %finish.1 = (f32[27,4,16]{2,1,0:T(4,128)}, f32[1,16]{1,0:T(1,128)}, f32[27,16,16]{2,1,0:T(8,128)}, f32[1,16]{1,0:T(1,128)}) custom-call(f32[16,8,128]{2,1,0:T(8,128)} %get-tuple-element.15.sums), custom_call_target="tpu_custom_call" | custom-call | tf_op jit(solution)/shard_map/finish/pallas_call | solution.py:451
  (1 shorter events, 0.0 us)
Async XLA Ops:
  0.6 0.7 copy-start.1
  1.3 0.7 copy-start.2
  69.5 1.8 %copy-start = (f32[8,8,8,128]{3,2,1,0:T(8,128)S(1)}, f32[8,8,8,128]{3,2,1,0:T(8,128)}, u32[]{:S(2)}) copy-start(f32[8,8,8,128]{3,2,1,0:T(8,128)} %get-tuple-element.14) | copy-start | bytes 786436

commit v4 on v3

--- a/solution.py
+++ b/solution.py
@@ -32,21 +32,42 @@
     return high, (value - high.astype(F32)).astype(BF)
 
 
-def pack_body(chunk, off, mass, vel, dest, out, acc):
-    blocks, _, slots = out.shape
-    count = off.shape[1]
+def rank_body(chunk, dest, codes, seats, blocks):
+    count, width = dest.shape[1], 256
     rows = iota((blocks, chunk), 0)
-    ranks = iota((slots, chunk), 0).astype(F32)
-    before = (iota((chunk, chunk), 0) < iota((chunk, chunk), 1)).astype(F32).astype(BF)
-    acc[...] = jnp.zeros_like(acc)
+    before = (iota((width, width), 0) < iota((width, width), 1)).astype(F32).astype(BF)
 
     def step(k, base):
         here = pl.ds(pl.multiple_of(k * chunk, chunk), chunk)
-        hot = (rows == dest[:, here]).astype(F32)
+        to = dest[:, here]
+        hot = (rows == to).astype(F32)
         hot16 = hot.astype(BF)
-        earlier = dot(hot16, before) + base
-        rank = jnp.sum(hot * earlier, axis=0, keepdims=True)
-        place = (ranks == rank).astype(F32).astype(BF)
+        ranks = []
+        for i in range(chunk // width):
+            cols = slice(i * width, (i + 1) * width)
+            earlier = dot(hot16[:, cols], before) + base
+            ranks.append(jnp.sum(hot[:, cols] * earlier, axis=0, keepdims=True))
+            base = base + jnp.sum(hot[:, cols], axis=1, keepdims=True)
+        rank = jnp.concatenate(ranks, axis=1).astype(jnp.int32)
+        codes[:, here] = to + (rank & 1) * blocks
+        seats[:, here] = rank >> 1
+        return base
+
+    lax.fori_loop(0, count // chunk, step, jnp.zeros((blocks, 1), F32))
+
+
+def pack_body(chunk, off, mass, vel, codes, seats, out, acc):
+    blocks, _, slots = out.shape
+    count, half = off.shape[1], slots // 2
+    rows = iota((2 * blocks, chunk), 0).astype(F32).astype(BF)
+    ranks = iota((half, chunk), 0).astype(F32).astype(BF)
+    one, zero = jnp.ones((), BF), jnp.zeros((), BF)
+    acc[...] = jnp.zeros_like(acc)
+
+    def step(k, carry):
+        here = pl.ds(pl.multiple_of(k * chunk, chunk), chunk)
+        hot = jnp.where(rows == codes[:, here].astype(F32).astype(BF), one, zero)
+        taken = ranks == seats[:, here].astype(F32).astype(BF)
         spot = off[:, here]
         m = mass[:, here]
         v = vel[:, here]
@@ -56,14 +77,19 @@
             + halves(spot[1:2] * 8.0)
             + (m.astype(BF), (m * v[0:1]).astype(BF), (m * v[1:2]).astype(BF), (m * v[2:3]).astype(BF))
         )
-        spread = jnp.concatenate([place * plane for plane in planes], axis=0)
-        acc[...] += dot(hot16, spread, NT)
-        return base + jnp.sum(hot, axis=1, keepdims=True)
-
-    lax.fori_loop(0, count // chunk, step, jnp.zeros((blocks, 1), F32))
+        spread = jnp.concatenate([jnp.where(taken, plane, zero) for plane in planes], axis=0)
+        acc[...] += dot(hot, spread, NT)
+        return carry
+
+    lax.fori_loop(0, count // chunk, step, 0)
+    low_half = iota((blocks, slots), 1) < half
 
     def plane(i):
-        return acc[:, i * slots : (i + 1) * slots]
+        cols = slice(i // 2 * slots, (i // 2 + 1) * slots)
+        even, odd = acc[:blocks, cols], acc[blocks:, cols]
+        if i % 2:
+            return jnp.where(low_half, pltpu.roll(even, half, 1), odd)
+        return jnp.where(low_half, even, pltpu.roll(odd, half, 1))
 
     for i in range(3):
         out[:, i, :] = plane(2 * i) + plane(2 * i + 1)
@@ -72,7 +98,7 @@
         out[:, 4 + i, :] = plane(6 + i)
 
 
-GROUP = 4
+GROUP = 16
 
 
 def hat(grid, at):
@@ -245,14 +271,17 @@
         inside = z_inside & ((at >= 0) & (at < ny * 8))
         dens[y] = jnp.where(inside, slab, 0.0).astype(BF)
 
+    diagonal = iota((16, 16), 0) == iota((16, 16), 1)
+
     def spread_bias(ref, times):
-        return jnp.concatenate([jnp.broadcast_to(ref[...], (16, 128))] * times, axis=0)
+        column = jnp.sum(jnp.where(diagonal, ref[...], 0.0), axis=1, keepdims=True)
+        return jnp.concatenate([jnp.broadcast_to(column, (16, 128))] * times, axis=0)
 
     bias1, bias2 = spread_bias(b1, 8), spread_bias(b2, 4)
 
     row1 = iota((128, 128), 0)
 
-    def conv1(by, carry):
+    def conv1(by):
         right = jnp.concatenate(
             [
                 jnp.concatenate([dens[2 * by + y, 16 * j : 16 * j + 32, :] for y in range(4)], axis=0)
@@ -272,16 +301,16 @@
             act[pl.ds(2 * by, 2), 4 * j : 4 * j + 4] = value.reshape(2, 4, 16, 128)
             slope = jnp.where(inside, sig * (1.0 + pre * (1.0 - sig)), 0.0)
             ds1[pl.ds(2 * by, 2), 4 * j : 4 * j + 4] = slope.reshape(2, 4, 16, 128)
-        return carry
-
-    lax.fori_loop(0, 7, conv1, 0)
+
+    for by in range(7):
+        conv1(by)
 
     def block(ref, y0, z0):
         return jnp.concatenate([ref[y0 + y, z0 : z0 + 4].reshape(64, 128) for y in range(4)], axis=0)
 
     row2 = iota((64, 128), 0)
 
-    def conv2(by, carry):
+    def conv2(by):
         right = jnp.concatenate([block(act, 2 * by, 2 * bz + 1) for bz in range(6)], axis=1)
         out = dot(t2[...], right)
         yy = gy * 8 + 2 * by - 2 + (row2 >> 5)
@@ -291,31 +320,26 @@
             sig = jax.nn.sigmoid(pre)
             zz = gz * 8 + 2 * bz - 2 + ((row2 >> 4) & 1)
             inside = y_in & (zz >= 0) & (zz < nz * 8)
-            if 1 <= bz <= 4:
-
-                @pl.when((by >= 1) & (by <= 4))
-                def _():
-                    refined[pl.ds(2 * by - 2, 2), 2 * bz - 2 : 2 * bz] = (
-                        (pre * sig).astype(BF).reshape(2, 2, 16, 128)
-                    )
+            if 1 <= bz <= 4 and 1 <= by <= 4:
+                refined[2 * by - 2 : 2 * by, 2 * bz - 2 : 2 * bz] = (pre * sig).reshape(2, 2, 16, 128)
 
             cot = cext[pl.ds(2 * by, 2), 2 * bz : 2 * bz + 2].reshape(64, 128).astype(F32)
             delta = jnp.where(inside, cot * (sig * (1.0 + pre * (1.0 - sig))), 0.0)
             d2[pl.ds(2 * by, 2), 2 * bz : 2 * bz + 2] = delta.astype(BF).reshape(2, 2, 16, 128)
-        return carry
-
-    lax.fori_loop(0, 6, conv2, 0)
-
-    def conv3(by, carry):
+
+    for by in range(6):
+        conv2(by)
+
+    def conv3(by):
         right = jnp.concatenate([block(d2, 2 * by, 2 * bz) for bz in range(5)], axis=1)
         out = dot(t2f[...], right)
         for bz in range(5):
             slope = ds1[pl.ds(2 * by + 2, 2), 2 * bz + 3 : 2 * bz + 5].reshape(64, 128)
             delta = along_x(out, 64, bz) * slope
             d1[pl.ds(2 * by, 2), 2 * bz : 2 * bz + 2] = delta.astype(BF).reshape(2, 2, 16, 128)
-        return carry
-
-    lax.fori_loop(0, 5, conv3, 0)
+
+    for by in range(5):
+        conv3(by)
 
     g2[...] = jnp.zeros_like(g2)
     g1[...] = jnp.zeros_like(g1)
@@ -323,7 +347,7 @@
     s1[...] = jnp.zeros_like(s1)
     table4 = t1f[...].astype(BF)
 
-    def last(by, carry):
+    def last(by):
         right = jnp.concatenate([block(d1, 2 * by, 2 * bz) for bz in range(4)], axis=1)
         out = dot(table4, right)
         for bz in range(4):
@@ -355,9 +379,9 @@
                 )
             )
         g1[...] += dot(jnp.concatenate(lefts, axis=1), jnp.concatenate(rights, axis=1), NT)
-        return carry
-
-    lax.fori_loop(0, 4, last, 0)
+
+    for by in range(4):
+        last(by)
 
     lane16 = iota((16, 128), 1)
     for x in range(3):
@@ -383,7 +407,7 @@
         sums[i] = jnp.zeros((8, 128), F32)
 
 
-def reduce_body(ny, nz, me_y, me_z, pay, out, from_z, from_y, send, receive):
+def reduce_body(ny, nz, me_y, me_z, pay, out, from_z, from_y, send, receive, meanwhile):
     def along_z(k):
         return (me_y, lax.rem(me_z + k, nz))
 
@@ -405,6 +429,7 @@
     ]
     for c in first:
         c.start()
+    meanwhile()
     for c in first:
         c.wait()
     total = pay[me_z]
@@ -427,7 +452,9 @@
         c.wait()
 
 
-def finish_body(scale, sums, first, bias1, second, bias2):
+def finish_body(scale, sums, refined, field, first, bias1, second, bias2, refined_out, field_out):
+    refined_out[...] = refined[...]
+    field_out[...] = field[...]
     kinds = [jnp.concatenate([sums[2 * i], sums[2 * i + 1]], axis=0) * scale for i in range(6)]
     turned = jnp.concatenate(kinds + [jnp.zeros((32, 128), F32)], axis=0).T
     for x in range(3):
@@ -447,7 +474,7 @@
     bias2[...] = turned[61:62, :16]
 
 
-def finish(sums, scale):
+def finish(scale, sums, refined, field):
     return pl.pallas_call(
         functools.partial(finish_body, scale),
         out_shape=[
@@ -455,20 +482,23 @@
             jax.ShapeDtypeStruct((1, 16), F32),
             jax.ShapeDtypeStruct((27, 16, 16), F32),
             jax.ShapeDtypeStruct((1, 16), F32),
+            jax.ShapeDtypeStruct(refined.shape, refined.dtype),
+            jax.ShapeDtypeStruct(field.shape, field.dtype),
         ],
-        in_specs=[VMEM],
-        out_specs=[VMEM] * 4,
+        in_specs=[VMEM] * 3,
+        out_specs=[VMEM] * 6,
         name="finish",
-    )(sums)
-
-
-GROUPS = 16
+    )(sums, refined, field)
+
+
+GROUPS = 8
 
 
 def step_body(ny, nz, off, mass, vel, dest, cot, w1, w2, b1, b2, refined, field, sums, *rest):
     (sent, pile, got, part, part16, cext, t1, t2, t2f, t1f, dens, act, ds1, d2, d1, g2, g1, s2, s1) = rest[:19]
     pieces, (pay, from_z, from_y) = rest[19:27], rest[27:30]
-    out_all, in_group, out_halo, in_halo, out_sum, in_sum = rest[30:]
+    codes, seats, wide, tall, deep = rest[30:35]
+    out_all, in_group, out_halo, in_halo, out_sum, in_sum = rest[35:]
     me_y, me_z = lax.axis_index("gy"), lax.axis_index("gz")
     devices = ny * nz
     size = devices // GROUPS
@@ -487,9 +517,13 @@
 
     lax.fori_loop(1, devices, greet, 0)
 
-    cext[2:10, 2:10] = cot[...]
+    for y in range(8):
+        plane = jnp.swapaxes(cot[:, y].astype(F32), 0, 1).astype(BF)
+        tall[y] = plane
+        cext[2 + y, 2:10] = plane
     tables_body(w1, w2, t1, t2, t2f, t1f)
-    pack_body(512, off, mass, vel, dest, sent, pile)
+    rank_body(2048, dest, codes, seats, devices)
+    pack_body(2048, off, mass, vel, codes, seats, sent, pile)
 
     pl.semaphore_wait(barrier, devices - 1)
 
@@ -523,7 +557,7 @@
     copies = [
         halo(
             8 + i,
-            cot.at[pl.ds(*C_FROM[a]), pl.ds(*C_FROM[b])],
+            tall.at[pl.ds(*C_FROM[a]), pl.ds(*C_FROM[b])],
             cext.at[pl.ds(C_INTO[a], C_FROM[a][1]), pl.ds(C_INTO[b], C_FROM[b][1])],
         )
         for i, (a, b) in enumerate(AROUND)
@@ -558,9 +592,15 @@
 
     unet_body(
         ny, nz, me_y, me_z, part, *pieces, cext, t1, t2, t2f, t1f, b1, b2,
-        refined, field, pay, dens, act, ds1, d2, d1, g2, g1, s2, s1,
+        wide, deep, pay, dens, act, ds1, d2, d1, g2, g1, s2, s1,
     )
-    reduce_body(ny, nz, me_y, me_z, pay, sums, from_z, from_y, out_sum, in_sum)
+
+    def turn():
+        for y in range(8):
+            refined[:, y] = jnp.swapaxes(wide[y], 0, 1).astype(BF)
+            field[:, y] = jnp.swapaxes(deep[y], 0, 1)[:4]
+
+    reduce_body(ny, nz, me_y, me_z, pay, sums, from_z, from_y, out_sum, in_sum, turn)
 
 
 def whole_step(ny, nz, slots, *args):
@@ -568,15 +608,15 @@
     return pl.pallas_call(
         functools.partial(step_body, ny, nz),
         out_shape=[
-            jax.ShapeDtypeStruct((8, 8, 16, 128), BF),
-            jax.ShapeDtypeStruct((8, 8, 8, 128), F32),
+            jax.ShapeDtypeStruct((16, 8, 8, 128), BF),
+            jax.ShapeDtypeStruct((4, 8, 8, 128), F32),
             jax.ShapeDtypeStruct((nz, 8, 128), F32),
         ],
         in_specs=[VMEM] * 9,
         out_specs=[VMEM] * 3,
         scratch_shapes=[
             pltpu.VMEM((devices, 8, slots), F32),
-            pltpu.VMEM((devices, 10 * slots), F32),
+            pltpu.VMEM((2 * devices, 5 * slots), F32),
             pltpu.VMEM((devices, 8, slots), F32),
             pltpu.VMEM((360, 128), F32),
             pltpu.VMEM((9, 40, 128), BF),
@@ -600,6 +640,11 @@
             pltpu.VMEM((nz, 8, 128), F32),
             pltpu.VMEM((nz, 8, 128), F32),
             pltpu.VMEM((ny, 8, 128), F32),
+            pltpu.VMEM((1, args[0].shape[1]), jnp.int32),
+            pltpu.VMEM((1, args[0].shape[1]), jnp.int32),
+            pltpu.VMEM((8, 8, 16, 128), F32),
+            pltpu.VMEM((8, 8, 16, 128), BF),
+            pltpu.VMEM((8, 8, 8, 128), F32),
             pltpu.SemaphoreType.DMA,
             pltpu.SemaphoreType.DMA((GROUPS,)),
             pltpu.SemaphoreType.DMA((16,)),
@@ -625,16 +670,16 @@
         mass.reshape(1, count),
         vel,
         dest.reshape(1, count),
-        cot.transpose(1, 2, 0, 3),
+        cot,
         w1.transpose(2, 3, 4, 1, 0).reshape(27, 4, 16),
         w2.transpose(2, 3, 4, 0, 1).reshape(27, 16, 16),
-        b1.reshape(16, 1),
-        b2.reshape(16, 1),
+        b1.reshape(1, 16),
+        b2.reshape(1, 16),
     )
-    first, bias1, second, bias2 = finish(sums, scale)
+    first, bias1, second, bias2, refined, field = finish(scale, sums, refined, field)
     return (
-        refined.transpose(2, 0, 1, 3),
-        field[:, :, :4].transpose(2, 0, 1, 3),
+        refined,
+        field,
         first.reshape(3, 3, 3, 4, 16).transpose(4, 3, 0, 1, 2),
         bias1.reshape(16),
         second.reshape(3, 3, 3, 16, 16).transpose(3, 4, 0, 1, 2),

time: 74 us -> 53.4 us (0.72)
  Pallas kernels: 66.8 us -> 52.6 us
  local copies, waits for them, and re-layouts: 6.29 us -> 0 us
    pallas_call x1, Pallas kernels: 65.1 us -> 50.6 us  [whole_step(): pl.pallas_call(functools.partial(step_body, ny, nz), out_shape=[jax.Shape...]
    unnamed x9 -> x0, local copies, waits for them, and re-layouts: 4.91 us -> none
    reshape x2 -> x0, local copies, waits for them, and re-layouts: 1.36 us -> none  [the longest x1 0.68 us: local(): b2.reshape(16, 1)]
where the time goes in v4:
time: 53.4 us; the launch traced here: 53.2 us
  Pallas kernels  52.6 us (99%)
  between operations  0.64 us (1%)
    pallas_call x1, Pallas kernels, whole_step(): pl.pallas_call(functools.partial(step_body, ny, nz), out_shape=[jax.Shape...  50.6 us
    pallas_call x1, Pallas kernels, finish(): pl.pallas_call(functools.partial(finish_body, scale), out_shape=[jax.Shap...  1.97 us

profile of v4, /device:TPU:1, one launch (start us, length us, event | category | flops | bytes accessed | tf_op | source)
XLA Modules:
  0.0 53.2 jit_solution(15123947357924021005)
XLA Ops:
  0.6 50.6 %step.1 = (bf16[16,8,8,128]{3,2,1,0:T(8,128)(2,1)}, f32[4,8,8,128]{3,2,1,0:T(8,128)}, f32[16,8,128]{2,1,0:T(8,128)}) custom-call(f32[3,8192]{1,0:T(4,128)} %off.1, f32[1,8192]{1,0:T(1,128)} %bitcast.19, f32[3,8192]{1,0:T(4,128)} %vel.1, s32[1,8192]{1,0:T(1,128)} %bitcast.20, bf16[16,8,8,128]{3,2,1,0:T(8,128)(2,1)} %cot.1, bf16[27,4,16]{2,1,0:T(4,128)(2,1)} %bitcast.21, ...), custom_call_target="tpu_custom_call" | custom-call | tf_op jit(solution)/shard_map/step/pallas_call | solution.py:608
  51.3 2.0 %finish.1 = (f32[27,4,16]{2,1,0:T(4,128)}, f32[1,16]{1,0:T(1,128)}, f32[27,16,16]{2,1,0:T(8,128)}, f32[1,16]{1,0:T(1,128)}, bf16[16,8,8,128]{3,2,1,0:T(8,128)(2,1)}, /*index=5*/f32[4,8,8,128]{3,2,1,0:T(8,128)}) custom-call(f32[16,8,128]{2,1,0:T(8,128)} %get-tuple-element.15.sums, bf16[16,8,8,128]{3,2,1,0:T(8,128)(2,1)} %get-tuple-element.16.refined, ...), custom_call_target="tpu_custom_call" | custom-call | tf_op jit(solution)/shard_map/finish/pallas_call | solution.py:478

commit v5 on v4

--- a/solution.py
+++ b/solution.py
@@ -498,7 +498,7 @@
     (sent, pile, got, part, part16, cext, t1, t2, t2f, t1f, dens, act, ds1, d2, d1, g2, g1, s2, s1) = rest[:19]
     pieces, (pay, from_z, from_y) = rest[19:27], rest[27:30]
     codes, seats, wide, tall, deep = rest[30:35]
-    out_all, in_group, out_halo, in_halo, out_sum, in_sum = rest[35:]
+    out_all, in_group, out_halo, in_halo, out_sum, in_sum, rows_in = rest[35:]
     me_y, me_z = lax.axis_index("gy"), lax.axis_index("gz")
     devices = ny * nz
     size = devices // GROUPS
@@ -511,21 +511,23 @@
     def device(a, b):
         return (lax.rem(me_y + a + ny, ny), lax.rem(me_z + b + nz, nz))
 
-    def greet(j, carry):
-        pl.semaphore_signal(barrier, inc=1, device_id=partner(j), device_id_type=MESH)
-        return carry
-
-    lax.fori_loop(1, devices, greet, 0)
+    row = [(me_y, lax.rem(me_z + k, nz)) for k in range(1, nz)]
+    column = [(lax.rem(me_y + k, ny), me_z) for k in range(1, ny)]
+    for to in row + column:
+        pl.semaphore_signal(barrier, inc=1, device_id=to, device_id_type=MESH)
 
     for y in range(8):
         plane = jnp.swapaxes(cot[:, y].astype(F32), 0, 1).astype(BF)
         tall[y] = plane
         cext[2 + y, 2:10] = plane
     tables_body(w1, w2, t1, t2, t2f, t1f)
+    pl.semaphore_wait(barrier, nz + ny - 2)
+    for to in column:
+        pl.semaphore_signal(rows_in, inc=1, device_id=to, device_id_type=MESH)
     rank_body(2048, dest, codes, seats, devices)
     pack_body(2048, off, mass, vel, codes, seats, sent, pile)
 
-    pl.semaphore_wait(barrier, devices - 1)
+    pl.semaphore_wait(rows_in, ny - 1)
 
     def send(j, carry):
         y, z = partner(j)
@@ -651,6 +653,7 @@
             pltpu.SemaphoreType.DMA((16,)),
             pltpu.SemaphoreType.DMA((2 * nz + ny,)),
             pltpu.SemaphoreType.DMA((2 * nz + ny,)),
+            pltpu.SemaphoreType.REGULAR,
         ],
         compiler_params=pltpu.CompilerParams(collective_id=1, has_side_effects=True, vmem_limit_bytes=LIMIT),
         name="step",

time: 53.4 us -> 53.8 us (level)
  no operation moved by 1% of the time
where the time goes in v5:
time: 53.8 us; the launch traced here: 53.6 us
  Pallas kernels  53 us (99%)
  between operations  0.64 us (1%)
    pallas_call x1, Pallas kernels, whole_step(): pl.pallas_call(functools.partial(step_body, ny, nz), out_shape=[jax.Shape...  51 us
    pallas_call x1, Pallas kernels, finish(): pl.pallas_call(functools.partial(finish_body, scale), out_shape=[jax.Shap...  1.97 us

profile of v5, /device:TPU:1, one launch (start us, length us, event | category | flops | bytes accessed | tf_op | source)
XLA Modules:
  0.0 53.6 jit_solution(12197077671620199240)
XLA Ops:
  0.6 51.0 %step.1 = (bf16[16,8,8,128]{3,2,1,0:T(8,128)(2,1)}, f32[4,8,8,128]{3,2,1,0:T(8,128)}, f32[16,8,128]{2,1,0:T(8,128)}) custom-call(f32[3,8192]{1,0:T(4,128)} %off.1, f32[1,8192]{1,0:T(1,128)} %bitcast.19, f32[3,8192]{1,0:T(4,128)} %vel.1, s32[1,8192]{1,0:T(1,128)} %bitcast.20, bf16[16,8,8,128]{3,2,1,0:T(8,128)(2,1)} %cot.1, bf16[27,4,16]{2,1,0:T(4,128)(2,1)} %bitcast.21, ...), custom_call_target="tpu_custom_call" | custom-call | tf_op jit(solution)/shard_map/step/pallas_call | solution.py:610
  51.6 2.0 %finish.1 = (f32[27,4,16]{2,1,0:T(4,128)}, f32[1,16]{1,0:T(1,128)}, f32[27,16,16]{2,1,0:T(8,128)}, f32[1,16]{1,0:T(1,128)}, bf16[16,8,8,128]{3,2,1,0:T(8,128)(2,1)}, /*index=5*/f32[4,8,8,128]{3,2,1,0:T(8,128)}) custom-call(f32[16,8,128]{2,1,0:T(8,128)} %get-tuple-element.15.sums, bf16[16,8,8,128]{3,2,1,0:T(8,128)(2,1)} %get-tuple-element.16.refined, ...), custom_call_target="tpu_custom_call" | custom-call | tf_op jit(solution)/shard_map/finish/pallas_call | solution.py:478

commit v6 on v5

--- a/solution.py
+++ b/solution.py
@@ -400,11 +400,13 @@
         if x == 0:
             low = jnp.where(lane16 == 60, jnp.sum(s1[...], axis=1, keepdims=True), low)
             low = jnp.where(lane16 == 61, jnp.sum(s2[...], axis=1, keepdims=True), low)
-        for half in range(2):
-            sums[2 * x + half] = low[8 * half : 8 * half + 8]
-            sums[6 + 2 * x + half] = high[8 * half : 8 * half + 8]
-    for i in range(12, 16):
-        sums[i] = jnp.zeros((8, 128), F32)
+        sums[x] = low
+        sums[3 + x] = high
+    sums[6] = jnp.zeros((16, 128), F32)
+    sums[7] = jnp.zeros((16, 128), F32)
+
+
+FAR_ROW = sorted(range(1, 16), key=lambda k: -min(k // 4, 4 - k // 4) - min(k % 4, 4 - k % 4))
 
 
 def reduce_body(ny, nz, me_y, me_z, pay, out, from_z, from_y, send, receive, meanwhile):
@@ -424,28 +426,26 @@
             device_id_type=MESH,
         )
 
-    first = [
-        copy(pay.at[lax.rem(me_z + k, nz)], from_z.at[k], k, along_z(k)) for k in range(1, nz)
-    ]
+    first = [copy(pay.at[lax.rem(me_y + k, ny)], from_y.at[k], k, along_y(k)) for k in range(1, ny)]
     for c in first:
         c.start()
     meanwhile()
     for c in first:
         c.wait()
-    total = pay[me_z]
-    for k in range(1, nz):
-        total = total + from_z[k]
-    from_y[me_y] = total
-    second = [copy(from_y.at[me_y], from_y.at[me_y], nz + k, along_y(k)) for k in range(1, ny)]
+    total = pay[me_y]
+    for k in range(1, ny):
+        total = total + from_y[k]
+    from_z[me_z] = total
+    second = [copy(from_z.at[me_z], from_z.at[me_z], ny + k, along_z(k)) for k in FAR_ROW]
     for c in second:
         c.start()
     for c in second:
         c.wait()
-    total = from_y[0]
-    for k in range(1, ny):
-        total = total + from_y[k]
-    out[me_z] = total
-    third = [copy(out.at[me_z], out.at[me_z], nz + ny + k, along_z(k)) for k in range(1, nz)]
+    total = from_z[0]
+    for k in range(1, nz):
+        total = total + from_z[k]
+    out[me_y] = total
+    third = [copy(out.at[me_y], out.at[me_y], nz + ny + k, along_y(k)) for k in range(1, ny)]
     for c in third:
         c.start()
     for c in third:
@@ -455,7 +455,7 @@
 def finish_body(scale, sums, refined, field, first, bias1, second, bias2, refined_out, field_out):
     refined_out[...] = refined[...]
     field_out[...] = field[...]
-    kinds = [jnp.concatenate([sums[2 * i], sums[2 * i + 1]], axis=0) * scale for i in range(6)]
+    kinds = [sums[i] * scale for i in range(6)]
     turned = jnp.concatenate(kinds + [jnp.zeros((32, 128), F32)], axis=0).T
     for x in range(3):
         for y in range(3):
@@ -516,15 +516,10 @@
     for to in row + column:
         pl.semaphore_signal(barrier, inc=1, device_id=to, device_id_type=MESH)
 
-    for y in range(8):
-        plane = jnp.swapaxes(cot[:, y].astype(F32), 0, 1).astype(BF)
-        tall[y] = plane
-        cext[2 + y, 2:10] = plane
-    tables_body(w1, w2, t1, t2, t2f, t1f)
+    rank_body(2048, dest, codes, seats, devices)
     pl.semaphore_wait(barrier, nz + ny - 2)
     for to in column:
         pl.semaphore_signal(rows_in, inc=1, device_id=to, device_id_type=MESH)
-    rank_body(2048, dest, codes, seats, devices)
     pack_body(2048, off, mass, vel, codes, seats, sent, pile)
 
     pl.semaphore_wait(rows_in, ny - 1)
@@ -544,6 +539,11 @@
     lax.fori_loop(1, devices, send, 0)
     got[0] = sent[me_y * nz + me_z]
 
+    for y in range(8):
+        plane = jnp.swapaxes(cot[:, y].astype(F32), 0, 1).astype(BF)
+        tall[y] = plane
+        cext[2 + y, 2:10] = plane
+
     def halo(i, src, dst):
         copy = pltpu.make_async_remote_copy(
             src_ref=src,
@@ -564,6 +564,8 @@
         )
         for i, (a, b) in enumerate(AROUND)
     ]
+
+    tables_body(w1, w2, t1, t2, t2f, t1f)
 
     def landed(first, count, g):
         pltpu.make_async_remote_copy(
@@ -612,7 +614,7 @@
         out_shape=[
             jax.ShapeDtypeStruct((16, 8, 8, 128), BF),
             jax.ShapeDtypeStruct((4, 8, 8, 128), F32),
-            jax.ShapeDtypeStruct((nz, 8, 128), F32),
+            jax.ShapeDtypeStruct((ny, 16, 128), F32),
         ],
         in_specs=[VMEM] * 9,
         out_specs=[VMEM] * 3,
@@ -639,9 +641,9 @@
         ]
         + [pltpu.VMEM((Y_PART[a][1], Z_PART[b][1], 128), BF) for a, b in AROUND]
         + [
-            pltpu.VMEM((nz, 8, 128), F32),
-            pltpu.VMEM((nz, 8, 128), F32),
-            pltpu.VMEM((ny, 8, 128), F32),
+            pltpu.VMEM((ny, 16, 128), F32),
+            pltpu.VMEM((nz, 16, 128), F32),
+            pltpu.VMEM((ny, 16, 128), F32),
             pltpu.VMEM((1, args[0].shape[1]), jnp.int32),
             pltpu.VMEM((1, args[0].shape[1]), jnp.int32),
             pltpu.VMEM((8, 8, 16, 128), F32),

time: 53.8 us -> 51.7 us (0.961)
  Pallas kernels: 53 us -> 50.9 us
    pallas_call x1, Pallas kernels: 51 us -> 49 us  [whole_step(): pl.pallas_call(functools.partial(step_body, ny, nz), out_shape=[jax.Shape...]
where the time goes in v6:
time: 51.7 us; the launch traced here: 51.6 us
  Pallas kernels  50.9 us (98%)
  between operations  0.64 us (1%)
    pallas_call x1, Pallas kernels, whole_step(): pl.pallas_call(functools.partial(step_body, ny, nz), out_shape=[jax.Shape...  49 us
    pallas_call x1, Pallas kernels, finish(): pl.pallas_call(functools.partial(finish_body, scale), out_shape=[jax.Shap...  1.97 us

profile of v6, /device:TPU:1, one launch (start us, length us, event | category | flops | bytes accessed | tf_op | source)
XLA Modules:
  0.0 51.6 jit_solution(14646339252309321010)
XLA Ops:
  0.6 49.0 %step.1 = (bf16[16,8,8,128]{3,2,1,0:T(8,128)(2,1)}, f32[4,8,8,128]{3,2,1,0:T(8,128)}, f32[8,16,128]{2,1,0:T(8,128)}) custom-call(f32[3,8192]{1,0:T(4,128)} %off.1, f32[1,8192]{1,0:T(1,128)} %bitcast.19, f32[3,8192]{1,0:T(4,128)} %vel.1, s32[1,8192]{1,0:T(1,128)} %bitcast.20, bf16[16,8,8,128]{3,2,1,0:T(8,128)(2,1)} %cot.1, bf16[27,4,16]{2,1,0:T(4,128)(2,1)} %bitcast.21, ...), custom_call_target="tpu_custom_call" | custom-call | tf_op jit(solution)/shard_map/step/pallas_call | solution.py:612
  49.6 2.0 %finish.1 = (f32[27,4,16]{2,1,0:T(4,128)}, f32[1,16]{1,0:T(1,128)}, f32[27,16,16]{2,1,0:T(8,128)}, f32[1,16]{1,0:T(1,128)}, bf16[16,8,8,128]{3,2,1,0:T(8,128)(2,1)}, /*index=5*/f32[4,8,8,128]{3,2,1,0:T(8,128)}) custom-call(f32[8,16,128]{2,1,0:T(8,128)} %get-tuple-element.15.sums, bf16[16,8,8,128]{3,2,1,0:T(8,128)(2,1)} %get-tuple-element.16.refined, ...), custom_call_target="tpu_custom_call" | custom-call | tf_op jit(solution)/shard_map/finish/pallas_call | solution.py:478
